TPU v7x, 1024 devices: a whole 4x4x32 slice. The times are simulated.
1024 devices in a mesh: grp: 8 (over y, core), seq: 32 (over z), rep: 4 (over x).
Axes of the slice: x: 4, y: 4, z: 32, core: 2. Of those that a mesh axis runs over, the one named last changes fastest.
Arguments:
- tokens: bfloat16 [131072, 2048], P(('rep', 'grp', 'seq')), parts along dimension 0, may hold values from -6 to 6
- token_cot: bfloat16 [131072, 2048], P(('rep', 'grp', 'seq')), parts along dimension 0, may hold values from -1.5 to 1.5
- router_logits: float32 [131072, 256], P(('rep', 'grp', 'seq')), parts along dimension 0, may hold values from -6 to 6
- token_lists: int32 [1024, 128], P('rep'), parts along dimension 0, may hold values from 0 to 32767, as said below
- w_gate: bfloat16 [256, 2048, 384], P(('grp', 'seq')), may hold values from -0.125 to 0.125
- w_up: bfloat16 [256, 2048, 384], P(('grp', 'seq')), may hold values from -0.125 to 0.125
- w_down: bfloat16 [256, 384, 2048], P(('grp', 'seq')), may hold values from -0.3125 to 0.3125
Outputs:
- token_grad: bfloat16 [131072, 2048], P(('rep', 'grp', 'seq')), parts along dimension 0
- logit_grad: float32 [131072, 256], P(('rep', 'grp', 'seq')), parts along dimension 0
There are 4 independent parts, one for each index of `rep`. A program takes and returns all parts, laid end to end along the dimension named above; an argument that names none is the same for every part. Nothing has to cross between parts.
Inputs may be any that keep to these rules, and one draw needn't show every extreme that they name: `token_lists`: row e lists 128 distinct tokens, no two of them from the same device's block of 128 consecutive tokens.
All inputs are finite; a program needn't handle non-finite values.
Results may differ from a plain program's by a relative error of at most 0.007.
Values may be sent and summed in bfloat16 or wider, within the bound.
A program may use at most 32 MiB of HBM per device.

v0:
```python
import jax
import jax.numpy as jnp
from jax import lax
from jax.sharding import PartitionSpec as P


def expert_back(in_rows, cot_rows, gate_mat, up_mat, down_mat):
    gate_pre = jnp.dot(in_rows, gate_mat, preferred_element_type=jnp.float32)
    up_pre = jnp.dot(in_rows, up_mat, preferred_element_type=jnp.float32)
    sig_gate = jax.nn.sigmoid(gate_pre)
    activated = gate_pre * sig_gate
    hidden = (activated * up_pre).astype(jnp.bfloat16)
    expert_out = jnp.dot(hidden, down_mat, preferred_element_type=jnp.float32)
    gate_grads = jnp.sum(cot_rows.astype(jnp.float32) * expert_out, axis=-1).astype(jnp.bfloat16)
    d_hidden = lax.dot_general(
        cot_rows, down_mat, (((1,), (1,)), ((), ())), preferred_element_type=jnp.float32
    )
    d_gate = (d_hidden * up_pre * sig_gate * (1.0 + gate_pre * (1.0 - sig_gate))).astype(
        jnp.bfloat16
    )
    d_up = (d_hidden * activated).astype(jnp.bfloat16)
    row_grads = lax.dot_general(
        d_gate, gate_mat, (((1,), (1,)), ((), ())), preferred_element_type=jnp.float32
    )
    row_grads = row_grads + lax.dot_general(
        d_up, up_mat, (((1,), (1,)), ((), ())), preferred_element_type=jnp.float32
    )
    return (row_grads.astype(jnp.bfloat16), gate_grads)


def body(tokens, token_cot, router_logits, token_lists, w_gate, w_up, w_down):
    n_groups = lax.axis_size("grp")
    n_columns = lax.axis_size("seq")
    own_index = lax.axis_index("grp") * n_columns + lax.axis_index("seq")
    tok_rows = tokens.shape[0]
    width = tokens.shape[1]
    n_experts = token_lists.shape[0]
    owners = token_lists // tok_rows
    is_mine = owners == own_index
    local_idx = token_lists - own_index * tok_rows
    listed = jnp.any(is_mine, axis=1)
    picked = jnp.sum(jnp.where(is_mine, local_idx, 0), axis=1)
    send_rows = jnp.where(listed[:, None], tokens[picked], jnp.zeros((), jnp.bfloat16))
    send_cots = jnp.where(listed[:, None], token_cot[picked], jnp.zeros((), jnp.bfloat16))
    send_rows = send_rows.reshape(n_groups, n_columns, width)
    send_cots = send_cots.reshape(n_groups, n_columns, width)
    arrived = (
        lax.all_to_all(send_rows, "seq", split_axis=1, concat_axis=1, tiled=True),
        lax.all_to_all(send_cots, "seq", split_axis=1, concat_axis=1, tiled=True),
    )
    in_rows = lax.all_to_all(arrived[0], "grp", split_axis=0, concat_axis=0, tiled=True)
    cot_rows = lax.all_to_all(arrived[1], "grp", split_axis=0, concat_axis=0, tiled=True)
    lead = in_rows.shape[:2]
    row_grads, gate_grads = expert_back(
        in_rows.reshape(-1, width), cot_rows.reshape(-1, width), w_gate[0], w_up[0], w_down[0]
    )
    row_grads, gate_grads = (row_grads.reshape(lead + (width,)), gate_grads.reshape(lead))
    back_rows = lax.all_to_all(row_grads, "grp", split_axis=0, concat_axis=0, tiled=True)
    back_gates = lax.all_to_all(gate_grads, "grp", split_axis=0, concat_axis=0, tiled=True)
    back_rows, back_gates = (
        lax.all_to_all(back_rows, "seq", split_axis=1, concat_axis=1, tiled=True),
        lax.all_to_all(back_gates, "seq", split_axis=1, concat_axis=1, tiled=True),
    )
    back_rows = back_rows.reshape(n_experts, width)
    back_gates = back_gates.reshape(n_experts).astype(jnp.float32)
    gate_vals = jax.nn.sigmoid(router_logits)
    expert_ids = jnp.arange(n_experts, dtype=jnp.int32)
    own_gates = gate_vals[picked, expert_ids] * listed.astype(jnp.float32)
    scaled = own_gates[:, None] * back_rows.astype(jnp.float32)
    select = (
        (picked[:, None] == jnp.arange(tok_rows, dtype=jnp.int32)[None, :]) & listed[:, None]
    ).astype(jnp.float32)
    token_grad = lax.dot_general(
        select,
        scaled,
        (((0,), (0,)), ((), ())),
        precision=lax.Precision.HIGHEST,
        preferred_element_type=jnp.float32,
    )
    logit_grad = jnp.transpose(select) * (gate_vals * (1.0 - gate_vals)) * back_gates[None, :]
    return (token_grad.astype(jnp.bfloat16), logit_grad)


def solution(mesh):
    in_specs = (
        P(("rep", "grp", "seq"), None),
        P(("rep", "grp", "seq"), None),
        P(("rep", "grp", "seq"), None),
        P("rep", None),
        P(("grp", "seq"), None, None),
        P(("grp", "seq"), None, None),
        P(("grp", "seq"), None, None),
    )
    out_specs = (P(("rep", "grp", "seq"), None), P(("rep", "grp", "seq"), None))
    return jax.shard_map(body, mesh=mesh, in_specs=in_specs, out_specs=out_specs, check_vma=False)
```

profile of v0, /device:TPU:1, one launch (start us, length us, event | category | flops | bytes accessed | tf_op | source)
XLA Modules:
  0.0 475.9 jit_solution(9127102903652390073)
XLA Ops:
  0.6 0.0 copy-start
  0.7 1.2 fusion.32
  1.8 0.1 broadcast_in_dim.20
  1.9 1.0 select_reduce_fusion
  3.0 0.1 copy.35
  3.1 0.0 copy-start.1
  3.1 3.5 gather_fusion.2
  6.6 0.0 copy-done.1
  6.6 2.3 gather_fusion.1
  9.0 5.2 %copy_select_fusion.1 = (bf16[8,32,2048]{2,0,1:T(8,128)(2,1)}, bf16[8,32,2048]{2,0,1:T(8,128)(2,1)S(1)}) fusion(bf16[8,32,2048]{2,1,0:T(8,128)(2,1)} %bitcast.39, pred[8,32]{0,1:T(8,128)(4,1)S(1)} %copy.35, bf16[8,32,2048]{2,1,0:T(8,128)(2,1)S(1)} %bitcast.38), kind=kLoop, calls=%fused_computation.20 | loop fusion | flops 1048576 | bytes 4194560 | tf_op jit(solution)/shard_map/jit(_where)/select_n | solution.py:44
  14.2 134.2 %all_to_all.45 = bf16[8,32,2048]{2,0,1:T(8,128)(2,1)} all-to-all(bf16[8,32,2048]{2,0,1:T(8,128)(2,1)S(1)} %get-tuple-element.9), channel_id=1, replica_groups=mesh['grp'=8,'seq'=32,'rep'=4] {'seq'}, dimensions={1} | all-to-all | bytes 2097152 | tf_op jit(solution)/shard_map/all_to_all | solution.py:48
  148.3 7.6 %all-to-all-start = ((bf16[8,32,2048]{2,0,1:T(8,128)(2,1)}), bf16[8,32,2048]{2,0,1:T(8,128)(2,1)S(1)}, u32[]{:S(2)}, u32[]{:S(2)}) async-start(bf16[8,32,2048]{2,0,1:T(8,128)(2,1)} %get-tuple-element.8), calls=%async_computation | async-start | bytes 2097152 | tf_op jit(solution)/shard_map/all_to_all | solution.py:49
  156.0 2.8 copy.39
  158.7 102.2 %all-to-all-done = bf16[8,32,2048]{2,0,1:T(8,128)(2,1)S(1)} async-done(((bf16[8,32,2048]{2,0,1:T(8,128)(2,1)}), bf16[8,32,2048]{2,0,1:T(8,128)(2,1)S(1)}, u32[]{:S(2)}, u32[]{:S(2)}) %all-to-all-start) | async-done | bytes 1048608 | tf_op jit(solution)/shard_map/all_to_all | solution.py:49
  260.9 0.0 copy-start.4
  260.9 1.0 copy-done.4
  261.9 5.5 %all-to-all-start.3 = ((bf16[8,32,2048]{2,1,0:T(8,128)(2,1)}), bf16[8,32,2048]{2,1,0:T(8,128)(2,1)S(1)}, u32[]{:S(2)}, u32[]{:S(2)}) async-start(bf16[8,32,2048]{2,1,0:T(8,128)(2,1)} %copy.39), calls=%async_computation.3 | async-start | bytes 2097152 | tf_op jit(solution)/shard_map/all_to_all | solution.py:51
  267.4 2.8 copy.37
  270.2 12.2 %all-to-all-done.3 = bf16[8,32,2048]{2,1,0:T(8,128)(2,1)S(1)} async-done(((bf16[8,32,2048]{2,1,0:T(8,128)(2,1)}), bf16[8,32,2048]{2,1,0:T(8,128)(2,1)S(1)}, u32[]{:S(2)}, u32[]{:S(2)}) %all-to-all-start.3) | async-done | bytes 1048608 | tf_op jit(solution)/shard_map/all_to_all | solution.py:51
  282.4 5.1 %all-to-all-start.1 = ((bf16[8,32,2048]{2,1,0:T(8,128)(2,1)}), bf16[8,32,2048]{2,1,0:T(8,128)(2,1)}, u32[]{:S(2)}, u32[]{:S(2)}) async-start(bf16[8,32,2048]{2,1,0:T(8,128)(2,1)} %copy.37), calls=%async_computation.1 | async-start | bytes 2097152 | tf_op jit(solution)/shard_map/all_to_all | solution.py:52
  287.5 0.0 copy-start.2
  287.5 0.0 copy-done
  287.5 0.7 fusion.3
  288.2 0.7 copy-done.2
  288.9 0.7 fusion.6
  289.6 13.0 %all-to-all-done.1 = bf16[8,32,2048]{2,1,0:T(8,128)(2,1)} async-done(((bf16[8,32,2048]{2,1,0:T(8,128)(2,1)}), bf16[8,32,2048]{2,1,0:T(8,128)(2,1)}, u32[]{:S(2)}, u32[]{:S(2)}) %all-to-all-start.1) | async-done | bytes 1048608 | tf_op jit(solution)/shard_map/all_to_all | solution.py:52
  302.6 0.0 copy-start.5
  302.6 2.6 fusion.9
  305.2 0.0 copy-done.5
  305.2 2.0 fusion.11
  307.2 0.7 convert_element_type.65
  307.9 4.2 all-to-all-start.6
  312.1 0.0 copy-start.3
  312.1 0.8 fusion.1
  312.9 0.6 copy-done.3
  313.5 1.7 fusion
  315.2 1.4 all-to-all-done.6
  316.6 4.2 all-to-all-start.4
  320.8 0.7 copy.43
  321.5 14.3 %all-to-all-done.4 = bf16[8,32,2048]{2,1,0:T(8,128)(2,1)S(1)} async-done(((bf16[8,32,2048]{2,1,0:T(8,128)(2,1)}), bf16[8,32,2048]{2,1,0:T(8,128)(2,1)S(1)}, u32[]{:S(2)}, u32[]{:S(2)}) %all-to-all-start.4) | async-done | bytes 1048608 | tf_op jit(solution)/shard_map/all_to_all | solution.py:58
  335.8 7.1 %all-to-all-start.7 = ((bf16[8,32,1]{0,2,1:T(2,128)(2,1)}), bf16[8,32,1]{0,2,1:T(2,128)(2,1)S(1)}, u32[]{:S(2)}, u32[]{:S(2)}) async-start(bf16[8,32,1]{0,2,1:T(2,128)(2,1)} %copy.43), calls=%async_computation.7 | async-start | bytes 32768 | tf_op jit(solution)/shard_map/all_to_all | solution.py:62
  342.9 1.6 copy.40
  344.5 0.0 copy-start.6
  344.5 19.6 %all-to-all-done.7 = bf16[8,32,1]{0,2,1:T(2,128)(2,1)S(1)} async-done(((bf16[8,32,1]{0,2,1:T(2,128)(2,1)}), bf16[8,32,1]{0,2,1:T(2,128)(2,1)S(1)}, u32[]{:S(2)}, u32[]{:S(2)}) %all-to-all-start.7) | async-done | bytes 544 | tf_op jit(solution)/shard_map/all_to_all | solution.py:62
  364.1 3.9 all-to-all-start.5
  368.0 0.1 copy.44
  368.1 0.1 reshape.79
  368.2 0.0 copy-done.6
  368.2 0.7 fusion.20
  368.9 2.3 gather_fusion
  371.3 102.1 %all-to-all-done.5 = bf16[8,32,2048]{2,0,1:T(8,128)(2,1)S(1)} async-done(((bf16[8,32,2048]{2,0,1:T(8,128)(2,1)}), bf16[8,32,2048]{2,0,1:T(8,128)(2,1)S(1)}, u32[]{:S(2)}, u32[]{:S(2)}) %all-to-all-start.5) | async-done | bytes 1048608 | tf_op jit(solution)/shard_map/all_to_all | solution.py:61
  473.4 0.6 copy.41
  474.0 1.9 convolution_convert_fusion
  (4 shorter events, 0.0 us)
Async XLA Ops:
  0.6 286.9 %copy-start = (bf16[1,2048,384]{2,1,0:T(8,128)(2,1)S(1)}, bf16[1,2048,384]{2,1,0:T(8,128)(2,1)}, u32[]{:S(2)}) copy-start(bf16[1,2048,384]{2,1,0:T(8,128)(2,1)} %param.11) | copy-start | bytes 4718596
  3.1 3.5 copy-start.1
  148.3 112.6 %all-to-all-start = ((bf16[8,32,2048]{2,0,1:T(8,128)(2,1)}), bf16[8,32,2048]{2,0,1:T(8,128)(2,1)S(1)}, u32[]{:S(2)}, u32[]{:S(2)}) async-start(bf16[8,32,2048]{2,0,1:T(8,128)(2,1)} %get-tuple-element.8), calls=%async_computation | async-start | bytes 2097152 | tf_op jit(solution)/shard_map/all_to_all | solution.py:49
  260.9 1.0 copy-start.4
  261.9 20.5 %all-to-all-start.3 = ((bf16[8,32,2048]{2,1,0:T(8,128)(2,1)}), bf16[8,32,2048]{2,1,0:T(8,128)(2,1)S(1)}, u32[]{:S(2)}, u32[]{:S(2)}) async-start(bf16[8,32,2048]{2,1,0:T(8,128)(2,1)} %copy.39), calls=%async_computation.3 | async-start | bytes 2097152 | tf_op jit(solution)/shard_map/all_to_all | solution.py:51
  282.4 20.2 %all-to-all-start.1 = ((bf16[8,32,2048]{2,1,0:T(8,128)(2,1)}), bf16[8,32,2048]{2,1,0:T(8,128)(2,1)}, u32[]{:S(2)}, u32[]{:S(2)}) async-start(bf16[8,32,2048]{2,1,0:T(8,128)(2,1)} %copy.37), calls=%async_computation.1 | async-start | bytes 2097152 | tf_op jit(solution)/shard_map/all_to_all | solution.py:52
  287.5 1.4 copy-start.2
  302.6 2.6 copy-start.5
  307.9 8.7 %all-to-all-start.6 = ((bf16[8,1,32]{2,1,0:T(2,128)(2,1)}), bf16[8,1,32]{2,1,0:T(2,128)(2,1)S(1)}, u32[]{:S(2)}, u32[]{:S(2)}) async-start(bf16[8,1,32]{2,1,0:T(2,128)(2,1)} %convert_element_type.65), calls=%async_computation.6 | async-start | bytes 8192 | tf_op jit(solution)/shard_map/all_to_all | solution.py:59
  312.1 1.4 copy-start.3
  316.6 19.2 %all-to-all-start.4 = ((bf16[8,32,2048]{2,1,0:T(8,128)(2,1)}), bf16[8,32,2048]{2,1,0:T(8,128)(2,1)S(1)}, u32[]{:S(2)}, u32[]{:S(2)}) async-start(bf16[8,32,2048]{2,1,0:T(8,128)(2,1)} %bitcast.41), calls=%async_computation.4 | async-start | bytes 2097152 | tf_op jit(solution)/shard_map/all_to_all | solution.py:58
  335.8 28.3 %all-to-all-start.7 = ((bf16[8,32,1]{0,2,1:T(2,128)(2,1)}), bf16[8,32,1]{0,2,1:T(2,128)(2,1)S(1)}, u32[]{:S(2)}, u32[]{:S(2)}) async-start(bf16[8,32,1]{0,2,1:T(2,128)(2,1)} %copy.43), calls=%async_computation.7 | async-start | bytes 32768 | tf_op jit(solution)/shard_map/all_to_all | solution.py:62
  344.5 23.7 %copy-start.6 = (f32[128,256]{1,0:T(8,128)S(1)}, f32[128,256]{1,0:T(8,128)}, u32[]{:S(2)}) copy-start(f32[128,256]{1,0:T(8,128)} %param.9) | copy-start | bytes 393220
  364.1 109.3 %all-to-all-start.5 = ((bf16[8,32,2048]{2,0,1:T(8,128)(2,1)}), bf16[8,32,2048]{2,0,1:T(8,128)(2,1)S(1)}, u32[]{:S(2)}, u32[]{:S(2)}) async-start(bf16[8,32,2048]{2,0,1:T(8,128)(2,1)} %copy.40), calls=%async_computation.5 | async-start | bytes 2097152 | tf_op jit(solution)/shard_map/all_to_all | solution.py:61
where the time goes:
time: 481 us; the launch traced here: 476 us
  waiting for transfers between devices  265 us (55%)
  blocking collectives  134 us (28%)
  starting transfers between devices  37.6 us (8%)
  local copies, waits for them, and re-layouts  19.9 us (4%)
  matrix products  10.5 us (2%)
  other arithmetic  8.14 us (2%)
    all_to_all x1, blocking collectives, body(): lax.all_to_all(send_rows, 'seq', split_axis=1, concat_axis=1, tiled=True)  134 us
    all_to_all x1, waiting for transfers between devices, body(): lax.all_to_all(send_cots, 'seq', split_axis=1, concat_axis=1, tiled=True)  102 us
    all_to_all x1, waiting for transfers between devices, body(): lax.all_to_all(back_rows, 'seq', split_axis=1, concat_axis=1, tiled=True)  102 us
    all_to_all x1, waiting for transfers between devices, body(): lax.all_to_all(back_gates, 'seq', split_axis=1, concat_axis=1, tiled=True)  19.6 us
    all_to_all x1, waiting for transfers between devices, body(): lax.all_to_all(row_grads, 'grp', split_axis=0, concat_axis=0, tiled=True)  14.3 us
    all_to_all x1, waiting for transfers between devices, body(): lax.all_to_all(arrived[1], 'grp', split_axis=0, concat_axis=0, tiled=True)  13 us
    all_to_all x1, waiting for transfers between devices, body(): lax.all_to_all(arrived[0], 'grp', split_axis=0, concat_axis=0, tiled=True)  12.2 us
  transfers between devices with their start and end apart: 7, of which 7 were waited for; matrix products, arithmetic and copies ran while one was open for 3% of the time, Pallas kernels for 0%

commit v1 on v0

v1 whole, which is shorter than its diff:
```python
import functools

import jax
import jax.numpy as jnp
from jax import lax
from jax.experimental import pallas as pl
from jax.experimental.pallas import tpu as pltpu
from jax.sharding import PartitionSpec as P

MESH = pl.DeviceIdType.MESH
BF16 = jnp.bfloat16
F32 = jnp.float32


def up16(n):
    return -(-n // 16) * 16


def one_hot_rows(pos_row, rows):
    row_ids = lax.broadcasted_iota(jnp.int32, (rows, pos_row.shape[1]), 0)
    return jnp.where(row_ids == pos_row, 1.0, 0.0).astype(BF16)


def ring_kernel(
    dims, caps,
    x_ref, g_ref, hot_ref, pos_ref, wg_hbm, wu_hbm, wd_hbm,
    fin_ref,
    wg_ref, wu_ref, wd_ref, send_buf, own, pack, final, gate_scr, up_scr, dxg, *rest,
):
    n_grp, n_seq, width, tail = dims
    half = n_seq // 2
    spc = half // 2
    wide = width + tail
    back = rest[:half]
    acc, back_send, w_sem, s1_send, s1_recv, d_send, d_recv, r_send, r_recv, s2_send, s2_recv, loc_sem = rest[half:]
    packs = (pack,) if not isinstance(pack, (tuple, list)) else pack
    lanes = n_grp * half
    grp = lax.axis_index("grp")
    col = lax.axis_index("seq")
    cap_last = caps[half - 1]

    def neighbour(direction):
        return lax.rem(col + 1 + direction * (n_seq - 2), n_seq)

    def peer(step):
        return lax.rem(grp + step, n_grp)

    weights = [
        pltpu.make_async_copy(wg_hbm, wg_ref, w_sem.at[0]),
        pltpu.make_async_copy(wu_hbm, wu_ref, w_sem.at[1]),
        pltpu.make_async_copy(wd_hbm, wd_ref, w_sem.at[2]),
    ]
    for copy in weights:
        copy.start()

    barrier = pltpu.get_barrier_semaphore()
    for step in range(1, n_grp):
        pl.semaphore_signal(barrier, inc=1, device_id={"grp": peer(step)}, device_id_type=MESH)
    for direction in range(2):
        pl.semaphore_signal(barrier, inc=1, device_id={"seq": neighbour(direction)}, device_id_type=MESH)

    col_tile = min(width, 512)
    n_tiles = width // col_tile

    def pick(source, arr, chunk):
        hot = hot_ref[pl.ds(chunk * lanes, lanes), :]

        def tile(i, carry):
            cols = pl.ds(pl.multiple_of(i * col_tile, col_tile), col_tile)
            rows = jnp.dot(hot, source[:, cols], preferred_element_type=F32).astype(BF16)
            send_buf[arr, chunk, :, :, cols] = rows.reshape(n_grp, half, col_tile)
            return carry

        lax.fori_loop(0, n_tiles, tile, 0)

    def stage_copy(arr, chunk, step):
        return pltpu.make_async_remote_copy(
            src_ref=send_buf.at[arr, chunk, peer(step)],
            dst_ref=own.at[arr, chunk, grp],
            send_sem=s1_send.at[arr, chunk, step],
            recv_sem=s1_recv.at[arr, chunk, step],
            device_id={"grp": peer(step)},
            device_id_type=MESH,
        )

    def stage_arrival(arr, chunk, step):
        return pltpu.make_async_remote_copy(
            src_ref=send_buf.at[arr, chunk, peer(step)],
            dst_ref=own.at[arr, chunk, lax.rem(grp + n_grp - step, n_grp)],
            send_sem=s1_send.at[arr, chunk, step],
            recv_sem=s1_recv.at[arr, chunk, step],
            device_id={"grp": peer(step)},
            device_id_type=MESH,
        )

    def stage_local(arr, chunk):
        return pltpu.make_async_copy(
            send_buf.at[arr, chunk, grp], own.at[arr, chunk, grp], loc_sem.at[arr, chunk]
        )

    pick(x_ref, 0, 0)
    pick(g_ref, 1, 0)
    pl.semaphore_wait(barrier, n_grp + 1)
    for chunk in range(2):
        for arr in range(2):
            if chunk == 1:
                pick((x_ref, g_ref)[arr], arr, chunk)
            stage_local(arr, chunk).start()
            for step in range(1, n_grp):
                stage_copy(arr, chunk, step).start()

    def own_rows(arr, chunk, cols):
        return own[arr, chunk, :, :, cols].reshape(lanes, col_tile)

    def packet(step):
        return packs[step]

    def send_packet(step, arr, direction):
        src = packet(step).at[arr, direction]
        if step + 1 < half:
            dst = packet(step + 1).at[arr, direction, pl.ds(0, caps[step])]
        else:
            dst = final.at[arr, pl.ds(direction * cap_last, cap_last)]
        return pltpu.make_async_remote_copy(
            src_ref=src,
            dst_ref=dst,
            send_sem=d_send.at[arr, direction, step],
            recv_sem=d_recv.at[arr, direction, step],
            device_id={"seq": neighbour(direction)},
            device_id_type=MESH,
        )

    for step in range(half):
        chunk = step // spc
        cap = caps[step]
        prev_cap = caps[step - 1] if step else 0
        for arr in range(2):
            if step % spc == 0:
                stage_local(arr, chunk).wait()
                for s in range(1, n_grp):
                    stage_arrival(arr, chunk, s).wait_recv()

            def hop(direction, carry, step=step, arr=arr, chunk=chunk, cap=cap, prev_cap=prev_cap):
                if step:
                    send_packet(step - 1, arr, direction).wait_recv()
                hot = one_hot_rows(pos_ref[pl.ds(2 * step + direction, 1), :], cap)

                def tile(i, inner):
                    cols = pl.ds(pl.multiple_of(i * col_tile, col_tile), col_tile)
                    rows = jnp.dot(hot, own_rows(arr, chunk, cols), preferred_element_type=F32)
                    target = packet(step)
                    if prev_cap:
                        held = target[arr, direction, pl.ds(0, prev_cap), cols].astype(F32)
                        target[arr, direction, pl.ds(0, prev_cap), cols] = (held + rows[:prev_cap]).astype(BF16)
                    if cap > prev_cap:
                        target[arr, direction, pl.ds(prev_cap, cap - prev_cap), cols] = rows[prev_cap:].astype(BF16)
                    return inner

                lax.fori_loop(0, n_tiles, tile, 0)
                send_packet(step, arr, direction).start()
                return carry

            lax.fori_loop(0, 2, hop, 0)

    for arr in range(2):
        hot = one_hot_rows(pos_ref[pl.ds(2 * half, 1), :], 16)

        def tile(i, inner, arr=arr, hot=hot):
            cols = pl.ds(pl.multiple_of(i * col_tile, col_tile), col_tile)
            rows = jnp.dot(hot, own_rows(arr, 0, cols), preferred_element_type=F32)
            final[arr, pl.ds(2 * cap_last, 16), cols] = rows.astype(BF16)
            return inner

        lax.fori_loop(0, n_tiles, tile, 0)

    for copy in weights:
        copy.wait()
    for direction in range(2):
        send_packet(half - 1, 0, direction).wait_recv()
    gate_scr[...] = jnp.dot(final[0], wg_ref[...], preferred_element_type=F32)
    up_scr[...] = jnp.dot(final[0], wu_ref[...], preferred_element_type=F32)
    for direction in range(2):
        send_packet(half - 1, 1, direction).wait_recv()
    nt = (((1,), (1,)), ((), ()))
    d_hidden = lax.dot_general(final[1], wd_ref[...], nt, preferred_element_type=F32)
    gate_pre = gate_scr[...]
    up_pre = up_scr[...]
    sig = jax.nn.sigmoid(gate_pre)
    activated = gate_pre * sig
    hidden = (activated * up_pre).astype(BF16).astype(F32)
    gate_grad = jnp.sum(hidden * d_hidden, axis=1, keepdims=True)
    d_gate = (d_hidden * up_pre * sig * (1.0 + gate_pre * (1.0 - sig))).astype(BF16)
    d_up = (d_hidden * activated).astype(BF16)
    gate_scr[...] = d_gate.astype(F32)
    up_scr[...] = d_up.astype(F32)
    dxg[:, width:] = jnp.broadcast_to(gate_grad, (gate_grad.shape[0], tail)).astype(BF16)

    def dx_tile(i, carry):
        cols = pl.ds(pl.multiple_of(i * col_tile, col_tile), col_tile)
        rows = lax.dot_general(gate_scr[...].astype(BF16), wg_ref[cols, :], nt, preferred_element_type=F32)
        rows = rows + lax.dot_general(up_scr[...].astype(BF16), wu_ref[cols, :], nt, preferred_element_type=F32)
        dxg[:, cols] = rows.astype(BF16)
        return carry

    lax.fori_loop(0, n_tiles, dx_tile, 0)

    def send_back(step, direction):
        cap = caps[half - 1 - step]
        if step == 0:
            src = dxg.at[pl.ds(direction * cap_last, cap_last)]
        else:
            src = back[step - 1].at[direction, pl.ds(0, cap)]
        return pltpu.make_async_remote_copy(
            src_ref=src,
            dst_ref=back[step].at[direction],
            send_sem=r_send.at[direction, step],
            recv_sem=r_recv.at[direction, step],
            device_id={"seq": neighbour(1 - direction)},
            device_id_type=MESH,
        )

    def home_copy(chunk, step, src_grp):
        return pltpu.make_async_remote_copy(
            src_ref=back_send.at[chunk, peer(step)],
            dst_ref=fin_ref.at[chunk, src_grp],
            send_sem=s2_send.at[chunk, step],
            recv_sem=s2_recv.at[chunk, step],
            device_id={"grp": peer(step)},
            device_id_type=MESH,
        )

    def home_local(chunk):
        return pltpu.make_async_copy(back_send.at[chunk, grp], fin_ref.at[chunk, grp], loc_sem.at[2, chunk])

    tn = (((0,), (0,)), ((), ()))

    def add_rows(chunk, hot, load):
        def tile(i, inner):
            cols = pl.ds(pl.multiple_of(i * col_tile, col_tile), col_tile)
            acc[:, cols] += lax.dot_general(hot, load(cols), tn, preferred_element_type=F32)
            return inner

        lax.fori_loop(0, n_tiles, tile, 0)
        last = pl.ds(width, tail)
        acc[:, last] += lax.dot_general(hot, load(last), tn, preferred_element_type=F32)

    for direction in range(2):
        send_back(0, direction).start()
    for step in range(half):
        chunk = 1 if step < spc else 0
        cap = caps[half - 1 - step]
        if step == 0:
            acc[...] = jnp.zeros_like(acc)
        if step == spc:
            acc[...] = jnp.zeros_like(acc)
            hot = one_hot_rows(pos_ref[pl.ds(2 * half, 1), :], 16)
            add_rows(0, hot, lambda cols: dxg[pl.ds(2 * cap_last, 16), cols])
        for direction in range(2):
            send_back(step, direction).wait_recv()
            if step + 1 < half:
                send_back(step + 1, direction).start()

        def drop(direction, carry, step=step, cap=cap, chunk=chunk):
            row = 2 * (half - 1 - step) + direction
            hot = one_hot_rows(pos_ref[pl.ds(row, 1), :], cap)
            add_rows(chunk, hot, lambda cols: back[step][direction, :, cols])
            return carry

        lax.fori_loop(0, 2, drop, 0)
        if step in (spc - 1, half - 1):
            back_send[chunk] = acc[...].astype(BF16).reshape(n_grp, half, wide)
            home_local(chunk).start()
            for s in range(1, n_grp):
                home_copy(chunk, s, grp).start()

    for chunk in range(2):
        home_local(chunk).wait()
        for s in range(1, n_grp):
            home_copy(chunk, s, lax.rem(grp + n_grp - s, n_grp)).wait_recv()
            home_copy(chunk, s, grp).wait_send()
        for arr in range(2):
            for s in range(1, n_grp):
                stage_copy(arr, chunk, s).wait_send()
    for step in range(half):
        for direction in range(2):
            for arr in range(2):
                send_packet(step, arr, direction).wait_send()
            send_back(step, direction).wait_send()


def entry(dims, caps, n_packs, *refs):
    ins, out, mid, rest = refs[:7], refs[7], refs[8:13], refs[13:]
    packs = rest[:n_packs]
    ring_kernel(dims, caps, *ins, out, *mid, packs, *rest[n_packs:])


def exchange(dims, caps, collective_id, tokens, token_cot, hot, pos, w_gate, w_up, w_down):
    n_grp, n_seq, width, tail = dims
    half = n_seq // 2
    ff = w_gate.shape[1]
    wide = width + tail
    rows = 2 * caps[-1] + 16
    lanes = n_grp * half
    dma = pltpu.SemaphoreType.DMA
    vmem = pl.BlockSpec(memory_space=pltpu.VMEM)
    hbm = pl.BlockSpec(memory_space=pl.ANY)
    scratch = [
        pltpu.VMEM(w_gate.shape, BF16),
        pltpu.VMEM(w_up.shape, BF16),
        pltpu.VMEM(w_down.shape, BF16),
        pltpu.VMEM((2, 2, n_grp, half, width), BF16),
        pltpu.VMEM((2, 2, n_grp, half, width), BF16),
        *[pltpu.VMEM((2, 2, cap, width), BF16) for cap in caps],
        pltpu.VMEM((2, rows, width), BF16),
        pltpu.VMEM((rows, ff), F32),
        pltpu.VMEM((rows, ff), F32),
        pltpu.VMEM((rows, wide), BF16),
        *[pltpu.VMEM((2, cap, wide), BF16) for cap in reversed(caps)],
        pltpu.VMEM((lanes, wide), F32),
        pltpu.VMEM((2, n_grp, half, wide), BF16),
        dma((3,)),
        dma((2, 2, n_grp)),
        dma((2, 2, n_grp)),
        dma((2, 2, half)),
        dma((2, 2, half)),
        dma((2, half)),
        dma((2, half)),
        dma((2, n_grp)),
        dma((2, n_grp)),
        dma((3, 2)),
    ]
    return pl.pallas_call(
        functools.partial(entry, dims, caps, half),
        out_shape=jax.ShapeDtypeStruct((2, n_grp, half, wide), BF16),
        in_specs=[vmem, vmem, vmem, vmem, hbm, hbm, hbm],
        out_specs=vmem,
        scratch_shapes=scratch,
        compiler_params=pltpu.CompilerParams(
            collective_id=collective_id, has_side_effects=True, vmem_limit_bytes=60 * 1024 * 1024
        ),
        name=f"ring_exchange_{collective_id}",
    )(tokens, token_cot, hot, pos, w_gate, w_up, w_down)


def to_slots(values, half):
    spc = half // 2
    first = jnp.concatenate(
        [jnp.flip(values[:, spc + 1 : half + 1], 1), values[:, :1], values[:, half + 1 : half + spc]], axis=1
    )
    second = jnp.concatenate([jnp.flip(values[:, 1 : spc + 1], 1), values[:, half + spc :]], axis=1)
    return jnp.stack([first, second])


def from_slots(slots, half):
    spc = half // 2
    first, second = slots[0], slots[1]
    return jnp.concatenate(
        [
            first[:, spc : spc + 1],
            jnp.flip(second[:, :spc], 1),
            jnp.flip(first[:, :spc], 1),
            first[:, spc + 1 :],
            second[:, spc:],
        ],
        axis=1,
    )


def roll_columns(values, start):
    doubled = jnp.concatenate([values, values], axis=1)
    return lax.dynamic_slice_in_dim(doubled, start, values.shape[1], axis=1)


def ring_positions(lists, tok_rows, n_grp, n_seq, col):
    half = n_seq // 2
    spc = half // 2
    owner = lists // tok_rows
    src = owner // n_seq
    off = lax.rem(owner % n_seq - col + n_seq, n_seq)
    here = off == 0
    dest = jnp.arange(n_seq, dtype=jnp.int32)[:, None]
    low = src < n_grp // 2
    d_up = lax.rem(dest - off + n_seq, n_seq)
    d_down = lax.rem(off - dest + n_seq, n_seq)
    in_up = (d_up < half) | ((d_up == half) & low)
    in_down = (d_down < half) | ((d_down == half) & ~low)
    groups = jnp.arange(n_grp, dtype=jnp.int32)

    def positions(inside, distance, own_distance):
        ahead = (inside & (distance > own_distance))[:, :, None]
        mine = (inside & here)[:, :, None]
        before = mine & (src[:, :, None] < groups)
        place = jnp.sum((ahead | before).astype(jnp.int32), axis=1)
        present = jnp.any(mine & (src[:, :, None] == groups), axis=1)
        return jnp.where(present, place, -1)

    up = jnp.flip(positions(in_up, d_up, dest)[1 : half + 1], 0)
    down = positions(in_down, d_down, n_seq - dest)[half:]
    by_step = jnp.stack([up, down], axis=1).reshape(n_seq, n_grp)
    same = jnp.any(here[0][:, None] & (src[0][:, None] == groups), axis=0)
    by_step = jnp.concatenate([by_step, jnp.where(same, groups, -1)[None, :]], axis=0)
    slot = [(k % spc) + spc * direction for k in range(half) for direction in range(2)]
    slot[1] = 0
    slot = jnp.array(slot + [spc], jnp.int32)
    at_slot = slot[:, None, None] == jnp.arange(half, dtype=jnp.int32)
    table = jnp.where(at_slot, by_step[:, :, None], -1).reshape(n_seq + 1, n_grp * half)
    return jnp.pad(table, ((0, 7), (0, 0)), constant_values=-1)


def body(tokens, token_cot, router_logits, token_lists, w_gate, w_up, w_down):
    n_grp = lax.axis_size("grp")
    n_seq = lax.axis_size("seq")
    half = n_seq // 2
    grp = lax.axis_index("grp")
    col = lax.axis_index("seq")
    tok_rows, width = tokens.shape
    n_experts, cap = token_lists.shape
    dims = (n_grp, n_seq, width, 128)

    token_ids = jnp.arange(tok_rows, dtype=jnp.int32)
    local = token_lists - (grp * n_seq + col) * tok_rows
    mine = (local >= 0) & (local < tok_rows)
    picked = jnp.max(jnp.where(mine, local, -1), axis=1)
    slots = to_slots(roll_columns(picked.reshape(n_grp, n_seq), col), half)
    hot = (slots.reshape(n_experts)[:, None] == token_ids).astype(BF16)

    ring_lists = lax.dynamic_slice_in_dim(token_lists, grp * n_seq, n_seq, axis=0)
    ring_lists = jnp.concatenate([ring_lists, ring_lists], axis=0)
    ring_lists = lax.dynamic_slice_in_dim(ring_lists, col, n_seq, axis=0)
    pos = ring_positions(ring_lists, tok_rows, n_grp, n_seq, col)

    full = tuple(up16(n_grp * k - n_grp // 2) for k in range(1, half + 1))
    fin = exchange(dims, full, 0, tokens, token_cot, hot, pos, w_gate[0], w_up[0], w_down[0])
    fin = fin.reshape(n_experts, width + dims[3])

    gate_vals = jax.nn.sigmoid(router_logits)
    select = picked[None, :] == token_ids[:, None]
    own_gates = jnp.sum(jnp.where(select, gate_vals, 0.0), axis=0)
    gate_slots = to_slots(roll_columns(own_gates.reshape(n_grp, n_seq), col), half).reshape(n_experts)
    weight = jnp.where(slots.reshape(n_experts)[:, None] == token_ids, gate_slots[:, None], 0.0)
    token_grad = lax.dot_general(
        weight,
        fin[:, :width].astype(F32),
        (((0,), (0,)), ((), ())),
        precision=lax.Precision.HIGHEST,
        preferred_element_type=F32,
    )
    back_gates = from_slots(fin[:, width].reshape(2, n_grp, half), half)
    back_gates = roll_columns(back_gates, lax.rem(n_seq - col, n_seq)).reshape(n_experts).astype(F32)
    logit_grad = jnp.where(select, gate_vals * (1.0 - gate_vals) * back_gates[None, :], 0.0)
    return (token_grad.astype(BF16), logit_grad)


def solution(mesh):
    in_specs = (
        P(("rep", "grp", "seq"), None),
        P(("rep", "grp", "seq"), None),
        P(("rep", "grp", "seq"), None),
        P("rep", None),
        P(("grp", "seq"), None, None),
        P(("grp", "seq"), None, None),
        P(("grp", "seq"), None, None),
    )
    out_specs = (P(("rep", "grp", "seq"), None), P(("rep", "grp", "seq"), None))
    return jax.shard_map(body, mesh=mesh, in_specs=in_specs, out_specs=out_specs, check_vma=False)
```

time: 481 us -> 405 us (0.84)
  Pallas kernels: 0 us -> 390 us
  waiting for transfers between devices: 265 us -> 0 us
  blocking collectives: 134 us -> 0 us
  starting transfers between devices: 37.6 us -> 0 us
  local copies, waits for them, and re-layouts: 19.9 us -> 4.51 us
  matrix products: 10.5 us -> 2.74 us
    pallas_call x0 -> x1, Pallas kernels: none -> 390 us  [exchange(): pl.pallas_call(functools.partial(entry, dims, caps, half), out_shape=jax....]
    all_to_all x7 -> x0, waiting for transfers between devices: 265 us -> none  [the longest x1 102 us: body(): lax.all_to_all(send_cots, 'seq', split_axis=1, concat_axis=1, tiled=True)]
    all_to_all x1 -> x0, blocking collectives: 134 us -> none  [body(): lax.all_to_all(send_rows, 'seq', split_axis=1, concat_axis=1, tiled=True)]
    all_to_all x7 -> x0, starting transfers between devices: 37.6 us -> none  [the longest x1 7.64 us: body(): lax.all_to_all(send_cots, 'seq', split_axis=1, concat_axis=1, tiled=True)]
    all_to_all x6 -> x0, local copies, waits for them, and re-layouts: 8.48 us -> none  [the longest x1 2.79 us: body(): lax.all_to_all(send_cots, 'seq', split_axis=1, concat_axis=1, tiled=True)]
    gather x3 -> x0, local copies, waits for them, and re-layouts: 8.21 us -> none  [the longest x1 3.54 us: body(): tokens[picked]]
    dot_general x7 -> x1, matrix products: 10.5 us -> 2.74 us  [body(): lax.dot_general(weight, fin[:, :width].astype(F32), (((0,), (0,)), ((), (...]
  transfers between devices with their start and end apart: 7 -> 0, of which waited for: 7 -> 0; matrix products, arithmetic and copies ran while one was open for 3% -> 0% of each run, Pallas kernels for 0% -> 0%
where the time goes in v1:
time: 405 us
  Pallas kernels  390 us (96%)
  other arithmetic  6.31 us (2%)
  local copies, waits for them, and re-layouts  4.51 us (1%)
    pallas_call x1, Pallas kernels, exchange(): pl.pallas_call(functools.partial(entry, dims, caps, half), out_shape=jax....  390 us

profile of v1, /device:TPU:1, one launch (start us, length us, event | category | flops | bytes accessed | tf_op | source)
XLA Modules:
  0.0 404.6 jit_solution(17107671697104356947)
XLA Ops:
  0.6 1.0 select_reduce_fusion.1
  1.7 0.7 iota_compare_fusion.6
  2.3 0.1 reshape.81
  2.4 0.1 pad_add_fusion.2
  2.5 0.1 constant_dynamic-slice_fusion.2
  2.6 0.1 slice.73
  2.6 0.1 fusion.33
  2.7 0.1 rev.25
  2.8 0.1 rev.26
  2.9 0.1 add_bitcast_fusion
  3.0 0.1 eq.49
  3.0 0.7 constant_dynamic-slice_fusion
  3.8 0.1 compare_and_fusion
  3.9 0.1 fusion.28
  4.0 0.1 copy.27
  4.1 1.2 fusion.9
  5.3 1.2 convert_reduce_fusion.1
  6.5 0.1 copy.24
  6.6 0.1 copy.23
  6.6 0.1 copy.25
  6.7 0.1 copy.26
  6.8 0.1 pad_add_fusion.3
  6.9 0.1 copy.28
  7.0 0.6 pad.4.refs_3_
  7.6 0.7 fusion.8.refs_2_
  8.3 0.0 copy-start
  8.3 390.3 %ring_exchange_0.1 = bf16[2,8,16,2176]{3,2,1,0:T(8,128)(2,1)} custom-call(bf16[128,2048]{1,0:T(8,128)(2,1)} %refs_0_.1, bf16[128,2048]{1,0:T(8,128)(2,1)} %refs_1_.1, bf16[256,128]{1,0:T(8,128)(2,1)} %fusion.8.refs_2_, s32[40,128]{1,0:T(8,128)} %pad.4.refs_3_, bf16[2048,384]{1,0:T(8,128)(2,1)} %bitcast.27, bf16[2048,384]{1,0:T(8,128)(2,1)} %bitcast.28, ...), custom_call_target="tpu_custom_call" | custom-call | tf_op jit(solution)/shard_map/ring_exchange_0/pallas_call | solution.py:332
  398.6 0.9 slice_reduce_fusion
  399.5 0.1 squeeze.19
  399.6 0.1 squeeze.18
  399.7 0.1 rev.31
  399.8 0.1 slice.91
  399.8 0.1 slice.87
  399.9 0.1 fusion.34
  400.0 0.1 rev.30
  400.1 0.1 concatenate.37
  400.2 0.1 dynamic-slice_convert_fusion
  400.3 0.1 reshape.85
  400.3 0.0 copy-done
  400.3 0.7 fusion.2
  401.1 0.1 reshape.82
  401.2 0.1 pad_maximum_fusion.1
  401.2 0.1 constant_dynamic-slice_fusion.1
  401.3 0.1 slice.78
  401.4 0.1 fusion.32
  401.5 0.1 rev.27
  401.5 0.1 maximum_bitcast_fusion
  401.6 0.1 rev.28
  401.7 0.1 maximum_bitcast_fusion.1
  401.8 0.1 broadcast_in_dim.77
  401.8 2.7 convolution_convert_fusion
  (13 shorter events, 0.1 us)
Async XLA Ops:
  8.3 392.0 %copy-start = (f32[128,256]{1,0:T(8,128)S(1)}, f32[128,256]{1,0:T(8,128)}, u32[]{:S(2)}) copy-start(f32[128,256]{1,0:T(8,128)} %param.10) | copy-start | bytes 393220

commit v2 on v1

v2 whole, which is shorter than its diff:
```python
import functools
import math

import jax
import jax.numpy as jnp
from jax import lax
from jax.experimental import pallas as pl
from jax.experimental.pallas import tpu as pltpu
from jax.sharding import PartitionSpec as P

MESH = pl.DeviceIdType.MESH
BF16 = jnp.bfloat16
F32 = jnp.float32


def up16(n):
    return -(-n // 16) * 16


def usual_caps(n_grp, n_seq):
    total = n_grp * n_seq
    caps = []
    for k in range(1, n_seq // 2 + 1):
        slots = n_grp * k - n_grp // 2
        spread = math.sqrt(slots * (total - slots) / (4 * total))
        caps.append(-(-math.floor(min(slots, slots / 2 + 4.75 * spread)) // 8) * 8)
    return tuple(max(cap, caps[0]) for cap in caps)


def one_hot_rows(pos_row, rows):
    row_ids = lax.broadcasted_iota(jnp.int32, (rows, pos_row.shape[1]), 0)
    return jnp.where(row_ids == pos_row, 1.0, 0.0).astype(BF16)


def ring_kernel(dims, caps, ins, fin_ref, scratch):
    n_grp, n_seq, width, tail = dims
    half = n_seq // 2
    spc = half // 2
    wide = width + tail
    lanes = n_grp * half
    x_ref, g_ref, hot_ref, pos_ref, src_pos_ref, wg_hbm, wu_hbm, wd_hbm = ins
    packs, backs = scratch["packs"], (scratch["backs_a"], scratch["backs_b"])
    wg_ref, wu_ref, wd_ref = scratch["wg"], scratch["wu"], scratch["wd"]
    send_buf, own, fresh, final = scratch["send_buf"], scratch["own"], scratch["fresh"], scratch["final"]
    gate_scr, up_scr, dx = scratch["gate"], scratch["up"], (scratch["dx_a"], scratch["dx_b"])
    dropped, back_send = scratch["dropped"], scratch["back_send"]
    parts = ((0, width // 2), (width // 2, wide - width // 2))
    grp = lax.axis_index("grp")
    col = lax.axis_index("seq")
    cap_last = caps[half - 1]
    col_tile = min(width // 2, 512)
    n_tiles = width // col_tile

    def tile_cols(i):
        return pl.ds(pl.multiple_of(i * col_tile, col_tile), col_tile)

    def neighbour(direction):
        return lax.rem(col + 1 + direction * (n_seq - 2), n_seq)

    def peer(step):
        return lax.rem(grp + step, n_grp)

    weights = [
        pltpu.make_async_copy(wg_hbm, wg_ref, scratch["w_sem"].at[0]),
        pltpu.make_async_copy(wu_hbm, wu_ref, scratch["w_sem"].at[1]),
        pltpu.make_async_copy(wd_hbm, wd_ref, scratch["w_sem"].at[2]),
    ]

    barrier = pltpu.get_barrier_semaphore()
    for step in range(1, n_grp):
        pl.semaphore_signal(barrier, inc=1, device_id={"grp": peer(step)}, device_id_type=MESH)
    for direction in range(2):
        pl.semaphore_signal(barrier, inc=1, device_id={"seq": neighbour(direction)}, device_id_type=MESH)

    def pick(source, arr, chunk):
        hot = hot_ref[pl.ds(chunk * lanes, lanes), :]

        def tile(i, carry):
            cols = tile_cols(i)
            rows = jnp.dot(hot, source[:, cols], preferred_element_type=F32).astype(BF16)
            send_buf[arr, chunk, :, :, cols] = rows.reshape(n_grp, half, col_tile)
            return carry

        lax.fori_loop(0, n_tiles, tile, 0)

    def stage_copy(arr, chunk, step, src_grp):
        return pltpu.make_async_remote_copy(
            src_ref=send_buf.at[arr, chunk, peer(step)],
            dst_ref=own.at[arr, chunk, src_grp],
            send_sem=scratch["s1_send"].at[arr, chunk, step],
            recv_sem=scratch["s1_recv"].at[arr, chunk, step],
            device_id={"grp": peer(step)},
            device_id_type=MESH,
        )

    def stage_local(arr, chunk):
        return pltpu.make_async_copy(
            send_buf.at[arr, chunk, grp], own.at[arr, chunk, grp], scratch["loc_sem"].at[arr, chunk]
        )

    def stage_wait(arr, chunk):
        stage_local(arr, chunk).wait()
        for step in range(1, n_grp):
            stage_copy(arr, chunk, step, lax.rem(grp + n_grp - step, n_grp)).wait_recv()

    pick(x_ref, 0, 0)
    pl.semaphore_wait(barrier, n_grp + 1)
    for chunk, arr in ((0, 0), (0, 1), (1, 0), (1, 1)):
        if chunk or arr:
            pick((x_ref, g_ref)[arr], arr, chunk)
        stage_local(arr, chunk).start()
        for step in range(1, n_grp):
            stage_copy(arr, chunk, step, grp).start()
    for copy in weights:
        copy.start()

    def send_packet(step, arr, direction):
        if step + 1 < half:
            dst = packs[step + 1].at[arr, direction, pl.ds(0, caps[step])]
        else:
            dst = final.at[arr, pl.ds(direction * cap_last, cap_last)]
        return pltpu.make_async_remote_copy(
            src_ref=packs[step].at[arr, direction],
            dst_ref=dst,
            send_sem=scratch["d_send"].at[arr, direction, step],
            recv_sem=scratch["d_recv"].at[arr, direction, step],
            device_id={"seq": neighbour(direction)},
            device_id_type=MESH,
        )

    def make_fresh(step, arr):
        cap = caps[step]
        prev_cap = caps[step - 1] if step else 0

        def one(direction, carry):
            hot = one_hot_rows(pos_ref[pl.ds(2 * step + direction, 1), :], cap)

            def tile(i, inner):
                cols = tile_cols(i)
                mine = own[arr, step // spc, :, :, cols].reshape(lanes, col_tile)
                rows = jnp.dot(hot, mine, preferred_element_type=F32).astype(BF16)
                if prev_cap:
                    fresh[arr, direction, pl.ds(0, prev_cap), cols] = rows[:prev_cap]
                if cap > prev_cap:
                    packs[step][arr, direction, pl.ds(prev_cap, cap - prev_cap), cols] = rows[prev_cap:]
                return inner

            lax.fori_loop(0, n_tiles, tile, 0)
            return carry

        lax.fori_loop(0, 2, one, 0)

    for step in range(half):
        for arr in range(2):
            if step == 0:
                stage_wait(arr, 0)
                make_fresh(0, arr)

            def hop(direction, carry, step=step, arr=arr):
                if step:
                    prev = pl.ds(0, caps[step - 1])
                    send_packet(step - 1, arr, direction).wait_recv()
                    packs[step][arr, direction, prev, :] += fresh[arr, direction, prev, :]
                send_packet(step, arr, direction).start()
                return carry

            lax.fori_loop(0, 2, hop, 0)
            if step + 1 < half:
                if step + 1 == spc:
                    stage_wait(arr, 1)
                make_fresh(step + 1, arr)

    same_hot = one_hot_rows(pos_ref[pl.ds(2 * half, 1), :], 16)
    for arr in range(2):

        def same_tile(i, inner, arr=arr):
            cols = tile_cols(i)
            mine = own[arr, 0, :, :, cols].reshape(lanes, col_tile)
            rows = jnp.dot(same_hot, mine, preferred_element_type=F32)
            final[arr, pl.ds(2 * cap_last, 16), cols] = rows.astype(BF16)
            return inner

        lax.fori_loop(0, n_tiles, same_tile, 0)

    for copy in weights:
        copy.wait()
    for direction in range(2):
        send_packet(half - 1, 0, direction).wait_recv()
    gate_scr[...] = jnp.dot(final[0], wg_ref[...], preferred_element_type=F32)
    up_scr[...] = jnp.dot(final[0], wu_ref[...], preferred_element_type=F32)
    for direction in range(2):
        send_packet(half - 1, 1, direction).wait_recv()
    nt = (((1,), (1,)), ((), ()))
    d_hidden = lax.dot_general(final[1], wd_ref[...], nt, preferred_element_type=F32)
    gate_pre = gate_scr[...]
    up_pre = up_scr[...]
    sig = jax.nn.sigmoid(gate_pre)
    activated = gate_pre * sig
    hidden = (activated * up_pre).astype(BF16).astype(F32)
    gate_grad = jnp.sum(hidden * d_hidden, axis=1, keepdims=True)
    scratch["d_gate"][...] = (d_hidden * up_pre * sig * (1.0 + gate_pre * (1.0 - sig))).astype(BF16)
    scratch["d_up"][...] = (d_hidden * activated).astype(BF16)
    dx[1][:, width // 2 :] = jnp.broadcast_to(gate_grad, (gate_grad.shape[0], tail)).astype(BF16)

    def send_back(step, part, direction):
        cap = caps[half - 1 - step]
        if step == 0:
            src = dx[part].at[pl.ds(direction * cap_last, cap_last)]
        else:
            src = backs[part][step - 1].at[direction, pl.ds(0, cap)]
        return pltpu.make_async_remote_copy(
            src_ref=src,
            dst_ref=backs[part][step].at[direction],
            send_sem=scratch["r_send"].at[part, direction, step],
            recv_sem=scratch["r_recv"].at[part, direction, step],
            device_id={"seq": neighbour(1 - direction)},
            device_id_type=MESH,
        )

    for part in range(2):

        def dx_tile(i, carry, part=part):
            w_rows = tile_cols(i + part * (n_tiles // 2))
            rows = lax.dot_general(scratch["d_gate"][...], wg_ref[w_rows, :], nt, preferred_element_type=F32)
            rows = rows + lax.dot_general(scratch["d_up"][...], wu_ref[w_rows, :], nt, preferred_element_type=F32)
            dx[part][:, tile_cols(i)] = rows.astype(BF16)
            return carry

        lax.fori_loop(0, n_tiles // 2, dx_tile, 0)
        for direction in range(2):
            send_back(0, part, direction).start()

    def home_copy(chunk, step, src_grp):
        return pltpu.make_async_remote_copy(
            src_ref=back_send.at[chunk, peer(step)],
            dst_ref=fin_ref.at[chunk, src_grp],
            send_sem=scratch["s2_send"].at[chunk, step],
            recv_sem=scratch["s2_recv"].at[chunk, step],
            device_id={"grp": peer(step)},
            device_id_type=MESH,
        )

    def home_local(chunk):
        return pltpu.make_async_copy(back_send.at[chunk, grp], fin_ref.at[chunk, grp], scratch["loc_sem"].at[2, chunk])

    tn = (((0,), (0,)), ((), ()))

    def drop(row, cap, rows, slot, part, add=False):
        hot = one_hot_rows(src_pos_ref[pl.ds(row, 1), :n_grp], cap)
        first, size = parts[part]
        kept = lax.dot_general(hot, rows, tn, preferred_element_type=F32)
        at = pl.ds(slot * n_grp, n_grp)
        if add:
            kept = kept + dropped[at, pl.ds(first, size)]
        dropped[at, pl.ds(first, size)] = kept

    def regroup(chunk):
        shape = (lanes, lanes)
        to = lax.broadcasted_iota(jnp.int32, shape, 0)
        frm = lax.broadcasted_iota(jnp.int32, shape, 1)
        perm = jnp.where((to // half == frm % n_grp) & (to % half == frm // n_grp), 1.0, 0.0).astype(BF16)

        def put(cols, size):
            rows = jnp.dot(perm, dropped[:, cols].astype(BF16), preferred_element_type=F32).astype(BF16)
            back_send[chunk, :, :, cols] = rows.reshape(n_grp, half, size)

        def tile(i, carry):
            put(tile_cols(i), col_tile)
            return carry

        lax.fori_loop(0, n_tiles, tile, 0)
        put(pl.ds(width, tail), tail)

    for step in range(half):
        chunk = 1 if step < spc else 0
        k = half - 1 - step
        for part in range(2):
            for direction in range(2):
                send_back(step, part, direction).wait_recv()
                if step + 1 < half:
                    send_back(step + 1, part, direction).start()
            if step == spc:
                drop(2 * half, 16, dx[part][pl.ds(2 * cap_last, 16), :], spc, part)
            for direction in range(2):
                slot = k % spc + (spc if direction and k else 0)
                drop(2 * k + direction, caps[k], backs[part][step][direction], slot, part, bool(direction and k == 0))
        if step in (spc - 1, half - 1):
            regroup(chunk)
            home_local(chunk).start()
            for s in range(1, n_grp):
                home_copy(chunk, s, grp).start()

    for arr in range(2):
        for chunk in range(2):
            for s in range(1, n_grp):
                stage_copy(arr, chunk, s, grp).wait_send()
    for step in range(half):
        for direction in range(2):
            for arr in range(2):
                send_packet(step, arr, direction).wait_send()
                send_back(step, arr, direction).wait_send()
    for chunk in (1, 0):
        home_local(chunk).wait()
        for s in range(1, n_grp):
            home_copy(chunk, s, grp).wait_send()
            home_copy(chunk, s, lax.rem(grp + n_grp - s, n_grp)).wait_recv()


N_INS = 8


def exchange(dims, caps, collective_id, *operands):
    n_grp, n_seq, width, tail = dims
    half = n_seq // 2
    w_gate, w_up, w_down = operands[5:]
    ff = w_gate.shape[1]
    wide = width + tail
    rows = 2 * caps[-1] + 16
    lanes = n_grp * half
    dma = pltpu.SemaphoreType.DMA
    vmem = pl.BlockSpec(memory_space=pltpu.VMEM)
    hbm = pl.BlockSpec(memory_space=pl.ANY)
    scratch = {
        "wg": pltpu.VMEM(w_gate.shape, BF16),
        "wu": pltpu.VMEM(w_up.shape, BF16),
        "wd": pltpu.VMEM(w_down.shape, BF16),
        "send_buf": pltpu.VMEM((2, 2, n_grp, half, width), BF16),
        "own": pltpu.VMEM((2, 2, n_grp, half, width), BF16),
        "packs": [pltpu.VMEM((2, 2, cap, width), BF16) for cap in caps],
        "fresh": pltpu.VMEM((2, 2, caps[-2], width), BF16),
        "final": pltpu.VMEM((2, rows, width), BF16),
        "gate": pltpu.VMEM((rows, ff), F32),
        "up": pltpu.VMEM((rows, ff), F32),
        "d_gate": pltpu.VMEM((rows, ff), BF16),
        "d_up": pltpu.VMEM((rows, ff), BF16),
        "dx_a": pltpu.VMEM((rows, width // 2), BF16),
        "dx_b": pltpu.VMEM((rows, wide - width // 2), BF16),
        "backs_a": [pltpu.VMEM((2, cap, width // 2), BF16) for cap in reversed(caps)],
        "backs_b": [pltpu.VMEM((2, cap, wide - width // 2), BF16) for cap in reversed(caps)],
        "dropped": pltpu.VMEM((lanes, wide), F32),
        "back_send": pltpu.VMEM((2, n_grp, half, wide), BF16),
        "w_sem": dma((3,)),
        "s1_send": dma((2, 2, n_grp)),
        "s1_recv": dma((2, 2, n_grp)),
        "d_send": dma((2, 2, half)),
        "d_recv": dma((2, 2, half)),
        "r_send": dma((2, 2, half)),
        "r_recv": dma((2, 2, half)),
        "s2_send": dma((2, n_grp)),
        "s2_recv": dma((2, n_grp)),
        "loc_sem": dma((3, 2)),
    }
    leaves, tree = jax.tree.flatten(scratch, is_leaf=lambda leaf: not isinstance(leaf, (dict, list)))

    def kernel(*refs):
        named = jax.tree.unflatten(tree, refs[N_INS + 1 :])
        ring_kernel(dims, caps, refs[:N_INS], refs[N_INS], named)

    return pl.pallas_call(
        kernel,
        out_shape=jax.ShapeDtypeStruct((2, n_grp, half, wide), BF16),
        in_specs=[vmem] * 5 + [hbm] * 3,
        out_specs=vmem,
        scratch_shapes=leaves,
        compiler_params=pltpu.CompilerParams(
            collective_id=collective_id, has_side_effects=True, vmem_limit_bytes=60 * 1024 * 1024
        ),
        name=f"ring_exchange_{collective_id}",
    )(*operands)


def to_slots(values, half):
    spc = half // 2
    first = jnp.concatenate(
        [jnp.flip(values[:, spc + 1 : half + 1], 1), values[:, :1], values[:, half + 1 : half + spc]], axis=1
    )
    second = jnp.concatenate([jnp.flip(values[:, 1 : spc + 1], 1), values[:, half + spc :]], axis=1)
    return jnp.stack([first, second])


def from_slots(slots, half):
    spc = half // 2
    first, second = slots[0], slots[1]
    return jnp.concatenate(
        [
            first[:, spc : spc + 1],
            jnp.flip(second[:, :spc], 1),
            jnp.flip(first[:, :spc], 1),
            first[:, spc + 1 :],
            second[:, spc:],
        ],
        axis=1,
    )


def roll_columns(values, start):
    doubled = jnp.concatenate([values, values], axis=1)
    return lax.dynamic_slice_in_dim(doubled, start, values.shape[1], axis=1)


def ring_positions(lists, tok_rows, n_grp, n_seq, col):
    half = n_seq // 2
    spc = half // 2
    owner = lists // tok_rows
    src = owner // n_seq
    off = (owner - col) & (n_seq - 1)
    here = off == 0
    dest = jnp.arange(n_seq, dtype=jnp.int32)[:, None]
    low = src < n_grp // 2
    d_up = (dest - off) & (n_seq - 1)
    d_down = (off - dest) & (n_seq - 1)
    in_up = (d_up < half) | ((d_up == half) & low)
    in_down = (d_down < half) | ((d_down == half) & ~low)
    groups = jnp.arange(n_grp, dtype=jnp.int32)

    def positions(inside, distance, own_distance):
        ahead = (inside & (distance > own_distance))[:, :, None]
        mine = (inside & here)[:, :, None]
        before = mine & (src[:, :, None] < groups)
        place = jnp.sum((ahead | before).astype(jnp.int32), axis=1)
        present = jnp.any(mine & (src[:, :, None] == groups), axis=1)
        return jnp.where(present, place, -1)

    up = jnp.flip(positions(in_up, d_up, dest)[1 : half + 1], 0)
    down = positions(in_down, d_down, n_seq - dest)[half:]
    by_step = jnp.stack([up, down], axis=1).reshape(n_seq, n_grp)
    same = jnp.any(here[0][:, None] & (src[0][:, None] == groups), axis=0)
    by_step = jnp.concatenate([by_step, jnp.where(same, groups, -1)[None, :]], axis=0)
    slot = [(k % spc) + spc * direction for k in range(half) for direction in range(2)]
    slot[1] = 0
    slot = jnp.array(slot + [spc], jnp.int32)
    at_slot = slot[:, None, None] == jnp.arange(half, dtype=jnp.int32)
    table = jnp.where(at_slot, by_step[:, :, None], -1).reshape(n_seq + 1, n_grp * half)
    return table, by_step


def lists_fit(lists, caps, tok_rows, n_grp, n_seq):
    half = n_seq // 2
    owner = lists // tok_rows
    low = owner // n_seq < n_grp // 2
    column = owner % n_seq
    dest = jnp.arange(lists.shape[0], dtype=jnp.int32)[:, None] % n_seq
    gap = (dest - column) & (n_seq - 1)
    d_up = jnp.where((gap < half) | ((gap == half) & low), gap, 0)
    gap = (column - dest) & (n_seq - 1)
    d_down = jnp.where((gap < half) | ((gap == half) & ~low), gap, 0)
    least = half - jnp.arange(half, dtype=jnp.int32)
    limit = jnp.array(caps, jnp.int32)
    worst = 0
    for distance in (d_up, d_down):
        count = jnp.sum((distance[:, None, :] >= least[:, None]).astype(jnp.int32), axis=2)
        worst = jnp.maximum(worst, jnp.max(count - limit))
    return worst <= 0


def body(tokens, token_cot, router_logits, token_lists, w_gate, w_up, w_down):
    n_grp = lax.axis_size("grp")
    n_seq = lax.axis_size("seq")
    half = n_seq // 2
    grp = lax.axis_index("grp")
    col = lax.axis_index("seq")
    tok_rows, width = tokens.shape
    n_experts, cap = token_lists.shape
    dims = (n_grp, n_seq, width, 128)

    token_ids = jnp.arange(tok_rows, dtype=jnp.int32)
    local = token_lists - (grp * n_seq + col) * tok_rows
    mine = (local >= 0) & (local < tok_rows)
    picked = jnp.max(jnp.where(mine, local, -1), axis=1)
    slots = to_slots(roll_columns(picked.reshape(n_grp, n_seq), col), half)
    hot = (slots.reshape(n_experts)[:, None] == token_ids).astype(BF16)

    ring_lists = lax.dynamic_slice_in_dim(token_lists, grp * n_seq, n_seq, axis=0)
    ring_lists = jnp.concatenate([ring_lists, ring_lists], axis=0)
    ring_lists = lax.dynamic_slice_in_dim(ring_lists, col, n_seq, axis=0)
    pos, src_pos = ring_positions(ring_lists, tok_rows, n_grp, n_seq, col)

    full = tuple(up16(n_grp * k - n_grp // 2) for k in range(1, half + 1))
    usual = usual_caps(n_grp, n_seq)
    fits = lists_fit(token_lists, usual, tok_rows, n_grp, n_seq)
    fits = jnp.full((8, 128), fits, F32)
    n_rep = lax.axis_size("rep")
    agreed = fits
    for shift in range(1, n_rep):
        agreed = agreed * lax.ppermute(fits, "rep", [(i, (i + shift) % n_rep) for i in range(n_rep)])
    fin = lax.cond(
        agreed[0, 0] > 0.5,
        functools.partial(exchange, dims, usual, 0),
        functools.partial(exchange, dims, full, 1),
        tokens, token_cot, hot, pos, src_pos, w_gate[0], w_up[0], w_down[0],
    )
    fin = fin.reshape(n_experts, width + dims[3])

    gate_vals = jax.nn.sigmoid(router_logits)
    select = picked[None, :] == token_ids[:, None]
    own_gates = jnp.sum(jnp.where(select, gate_vals, 0.0), axis=0)
    gate_slots = to_slots(roll_columns(own_gates.reshape(n_grp, n_seq), col), half).reshape(n_experts)
    weight = jnp.where(slots.reshape(n_experts)[:, None] == token_ids, gate_slots[:, None], 0.0)
    token_grad = lax.dot_general(
        weight,
        fin[:, :width].astype(F32),
        (((0,), (0,)), ((), ())),
        precision=lax.Precision.HIGHEST,
        preferred_element_type=F32,
    )
    back_gates = from_slots(fin[:, width].reshape(2, n_grp, half), half)
    back_gates = roll_columns(back_gates, lax.rem(n_seq - col, n_seq)).reshape(n_experts).astype(F32)
    logit_grad = jnp.where(select, gate_vals * (1.0 - gate_vals) * back_gates[None, :], 0.0)
    return (token_grad.astype(BF16), logit_grad)


def solution(mesh):
    in_specs = (
        P(("rep", "grp", "seq"), None),
        P(("rep", "grp", "seq"), None),
        P(("rep", "grp", "seq"), None),
        P("rep", None),
        P(("grp", "seq"), None, None),
        P(("grp", "seq"), None, None),
        P(("grp", "seq"), None, None),
    )
    out_specs = (P(("rep", "grp", "seq"), None), P(("rep", "grp", "seq"), None))
    return jax.shard_map(body, mesh=mesh, in_specs=in_specs, out_specs=out_specs, check_vma=False)
```

time: 405 us -> 313 us (0.77)
  Pallas kernels: 390 us -> 275 us
  starting transfers between devices: 0 us -> 10.8 us
  other arithmetic: 6.31 us -> 16.6 us
    pallas_call x1, Pallas kernels: 390 us -> 275 us  [exchange(): pl.pallas_call(kernel, out_shape=jax.ShapeDtypeStruct((2, n_grp, half, wi...]
    ppermute x0 -> x3, starting transfers between devices: none -> 10.8 us  [body(): lax.ppermute(fits, 'rep', [(i, (i + shift) % n_rep) for i in range(n_rep)])]
    reduce_sum x0 -> x1, other arithmetic: none -> 8.76 us  [lists_fit(): jnp.sum((distance[:, None, :] >= least[:, None]).astype(jnp.int32), axis=2)]
  transfers between devices with their start and end apart: 0 -> 3, of which waited for: 0 -> 0; matrix products, arithmetic and copies ran while one was open for 0% -> 1% of each run, Pallas kernels for 0% -> 0%
where the time goes in v2:
time: 313 us; the launch traced here: 312 us
  Pallas kernels  275 us (88%)
  other arithmetic  16.6 us (5%)
  starting transfers between devices  10.8 us (3%)
  local copies, waits for them, and re-layouts  5.08 us (2%)
    pallas_call x1, Pallas kernels, exchange(): pl.pallas_call(kernel, out_shape=jax.ShapeDtypeStruct((2, n_grp, half, wi...  275 us
    ppermute x3, starting transfers between devices, body(): lax.ppermute(fits, 'rep', [(i, (i + shift) % n_rep) for i in range(n_rep)])  10.8 us
    reduce_sum x1, other arithmetic, lists_fit(): jnp.sum((distance[:, None, :] >= least[:, None]).astype(jnp.int32), axis=2)  8.76 us
  transfers between devices with their start and end apart: 3, of which 0 were waited for; matrix products, arithmetic and copies ran while one was open for 1% of the time, Pallas kernels for 0%

profile of v2, /device:TPU:1, one launch (start us, length us, event | category | flops | bytes accessed | tf_op | source)
XLA Modules:
  0.0 312.5 jit_solution(6191858159207472368)
XLA Ops:
  0.6 0.0 copy-start.3
  0.7 1.3 or_select_fusion.1
  2.0 1.1 select_reduce_fusion.1
  3.1 8.8 %convert_reduce_fusion = (s32[256,16]{1,0:T(8,128)S(1)}, s32[256,16]{1,0:T(8,128)S(1)}) fusion(s32[256,128]{1,0:T(8,128)S(1)} %get-tuple-element.138, s32[16]{0:T(128)S(1)} %iota_subtract_fusion.1, s32[256,128]{1,0:T(8,128)S(1)} %get-tuple-element.133), kind=kLoop, calls=%fused_computation.1 | loop fusion | flops 3137536 | bytes 294976 | tf_op jit(solution)/shard_map/reduce_sum | solution.py:451
  11.9 0.1 copy.42
  12.0 0.1 copy.41
  12.0 1.4 add_reduce_fusion
  14.7 5.5 %collective-permute-start.1 = (f32[8,128]{1,0:T(8,128)S(1)}, f32[8,128]{1,0:T(8,128)S(1)}, u32[]{:S(2)}, u32[]{:S(2)}) collective-permute-start(f32[8,128]{1,0:T(8,128)S(1)} %broadcast_in_dim.90), channel_id=1, source_target_pairs={{0,2},{1,3},{2,0},{3,1},{4,6},{5,7},{6,4},{7,5},{8,10},{9,11},{10,... | collective-permute-start | bytes 12296 | tf_op jit(solution)/shard_map/ppermute | solution.py:485
  20.2 2.8 collective-permute-start.2
  23.0 2.5 collective-permute-start
  25.5 0.7 constant_dynamic-slice_fusion
  26.2 0.1 compare_and_fusion
  26.4 0.1 reshape.107
  26.4 0.1 pad_add_fusion.2
  26.5 0.1 constant_dynamic-slice_fusion.2
  26.6 0.1 slice.76
  26.7 0.1 fusion.36
  26.8 0.1 fusion.29
  26.9 0.1 copy.47
  27.0 1.2 fusion.13
  28.2 1.2 convert_reduce_fusion.3
  29.3 0.1 copy.44
  29.4 0.1 copy.43
  29.5 0.1 copy.45
  29.6 0.1 copy.46
  29.6 0.1 rev.25
  29.7 0.1 rev.26
  29.8 0.1 add_bitcast_fusion
  29.9 0.1 eq.55
  30.0 0.1 pad_add_fusion.3
  30.0 0.1 fusion.10
  30.2 0.0 collective-permute-done.1
  30.2 0.0 collective-permute-done.2
  30.2 0.0 collective-permute-done
  30.2 0.5 slice.84
  31.4 0.0 copy-done
  31.4 0.0 copy-start.2
  31.4 277.1 %conditional.1 = (bf16[2,8,16,2176]{3,2,1,0:T(8,128)(2,1)S(1)}) conditional(s32[]{:T(128)} %bitcast.4, (bf16[128,2048]{1,0:T(8,128)(2,1)S(1)}, bf16[128,2048]{1,0:T(8,128)(2,1)}, bf16[256,128]{1,0:T(8,128)(2,1)S(1)}, s32[33,128]{0,1:T(8,128)S(1)}, s32[33,8]{0,1:T(8,128)S(1)}, /*index=5*/bf16[2048,384]{1,0:T(8,128)(2,1)S(1)}, ...), branch_computations={%region_11.12_spmd, %region_12.13_spmd} | conditional | bytes 35912 | solution.py:486
  31.8 0.7 copy.51.refs_4_
  32.5 0.7 copy.50.refs_3_
  33.2 275.3 %ring_exchange_0.1 = bf16[2,8,16,2176]{3,2,1,0:T(8,128)(2,1)S(1)} custom-call(bf16[128,2048]{1,0:T(8,128)(2,1)S(1)} %get-tuple-element.43.refs_0_, bf16[128,2048]{1,0:T(8,128)(2,1)} %get-tuple-element.44.refs_1_, bf16[256,128]{1,0:T(8,128)(2,1)S(1)} %get-tuple-element.45.refs_2_, s32[33,128]{1,0:T(8,128)} %copy.50.refs_3_, s32[33,8]{1,0:T(8,128)} %copy.51.refs_4_, ...), custom_call_target="tpu_custom_call" | custom-call | tf_op jit(solution)/shard_map/cond/branch_1_fun/ring_exchange_0/pallas_call | solution.py:359
  308.5 0.1 slice_reduce_fusion
  308.6 0.1 squeeze.19
  308.7 0.1 slice.95
  308.8 0.1 slice.91
  308.9 0.1 squeeze.20
  308.9 0.1 rev.31
  309.0 0.1 fusion.37
  309.1 0.1 rev.30
  309.2 0.1 concatenate.37
  309.3 0.1 dynamic-slice_convert_fusion
  309.4 0.1 reshape.112
  309.5 0.7 fusion.4
  310.2 0.1 reshape.108
  310.3 0.1 pad_maximum_fusion.1
  310.4 0.1 constant_dynamic-slice_fusion.1
  310.4 0.1 slice.81
  310.5 0.1 fusion.35
  310.6 0.1 rev.27
  310.7 0.1 rev.28
  310.7 0.1 maximum_bitcast_fusion.1
  310.8 0.1 maximum_bitcast_fusion
  310.9 0.1 broadcast_in_dim.58
  311.0 1.5 convolution_convert_fusion
  (22 shorter events, 0.1 us)
Async XLA Ops:
  0.6 26.1 %copy-start.3 = (s32[33]{0:T(128)S(1)}, s32[33]{0:T(128)}, u32[]{:S(2)}) copy-start(s32[33]{0:T(128)} %constant.112.clone) | copy-start | bytes 400
  0.6 30.7 %copy-start = (bf16[1,2048,384]{2,1,0:T(8,128)(2,1)S(1)}, bf16[1,2048,384]{2,1,0:T(8,128)(2,1)}, u32[]{:S(2)}) copy-start(bf16[1,2048,384]{2,1,0:T(8,128)(2,1)} %param.15) | copy-start | bytes 4718596
  0.7 30.7 %copy-start.1 = (bf16[128,2048]{1,0:T(8,128)(2,1)S(1)}, bf16[128,2048]{1,0:T(8,128)(2,1)}, u32[]{:S(2)}) copy-start(bf16[128,2048]{1,0:T(8,128)(2,1)} %param.11) | copy-start | bytes 1572868
  14.7 15.5 %collective-permute-start.1 = (f32[8,128]{1,0:T(8,128)S(1)}, f32[8,128]{1,0:T(8,128)S(1)}, u32[]{:S(2)}, u32[]{:S(2)}) collective-permute-start(f32[8,128]{1,0:T(8,128)S(1)} %broadcast_in_dim.90), channel_id=1, source_target_pairs={{0,2},{1,3},{2,0},{3,1},{4,6},{5,7},{6,4},{7,5},{8,10},{9,11},{10,... | collective-permute-start | bytes 12296 | tf_op jit(solution)/shard_map/ppermute | solution.py:485
  20.2 10.0 %collective-permute-start.2 = (f32[8,128]{1,0:T(8,128)S(1)}, f32[8,128]{1,0:T(8,128)S(1)}, u32[]{:S(2)}, u32[]{:S(2)}) collective-permute-start(f32[8,128]{1,0:T(8,128)S(1)} %broadcast_in_dim.90), channel_id=1, source_target_pairs={{0,3},{1,0},{2,1},{3,2},{4,7},{5,4},{6,5},{7,6},{8,11},{9,8},{10,9... | collective-permute-start | bytes 12296 | tf_op jit(solution)/shard_map/ppermute | solution.py:485
  23.0 7.2 %collective-permute-start = (f32[8,128]{1,0:T(8,128)S(1)}, f32[8,128]{1,0:T(8,128)S(1)}, u32[]{:S(2)}, u32[]{:S(2)}) collective-permute-start(f32[8,128]{1,0:T(8,128)S(1)} %broadcast_in_dim.90), channel_id=1, source_target_pairs={{0,1},{1,2},{2,3},{3,0},{4,5},{5,6},{6,7},{7,4},{8,9},{9,10},{10,1... | collective-permute-start | bytes 12296 | tf_op jit(solution)/shard_map/ppermute | solution.py:485
  31.4 278.1 %copy-start.2 = (f32[128,256]{1,0:T(8,128)S(1)}, f32[128,256]{1,0:T(8,128)}, u32[]{:S(2)}) copy-start(f32[128,256]{1,0:T(8,128)} %param.13) | copy-start | bytes 393220

commit v3 on v2

--- a/solution.py
+++ b/solution.py
@@ -398,93 +398,184 @@
     return lax.dynamic_slice_in_dim(doubled, start, values.shape[1], axis=1)
 
 
-def ring_positions(lists, tok_rows, n_grp, n_seq, col):
+def prepare_kernel(dims, tok_rows, caps, lists_ref, flag_ref, picked_ref, hot_ref, pos_ref, src_pos_ref, got, send_sem, recv_sem):
+    n_grp, n_seq, n_rep = dims
     half = n_seq // 2
     spc = half // 2
-    owner = lists // tok_rows
-    src = owner // n_seq
-    off = (owner - col) & (n_seq - 1)
-    here = off == 0
-    dest = jnp.arange(n_seq, dtype=jnp.int32)[:, None]
+    lanes = n_grp * half
+    n_experts = lists_ref.shape[0]
+    rep, grp, col = lax.axis_index("rep"), lax.axis_index("grp"), lax.axis_index("seq")
+    me = grp * n_seq + col
+
+    def peer(step):
+        return lax.rem(rep + step, n_rep)
+
+    barrier = pltpu.get_barrier_semaphore()
+    for step in range(1, n_rep):
+        pl.semaphore_signal(barrier, inc=1, device_id={"rep": peer(step)}, device_id_type=MESH)
+
+    def iota(shape, axis):
+        return lax.broadcasted_iota(jnp.int32, shape, axis)
+
+    def shift(n):
+        return n.bit_length() - 1
+
+    lists = jnp.transpose(lists_ref[...])
+    owner = lists >> shift(tok_rows)
+    src = owner >> shift(n_seq)
+    column = owner & (n_seq - 1)
+    expert = iota((1, n_experts), 1)
+    dest = expert & (n_seq - 1)
     low = src < n_grp // 2
-    d_up = (dest - off) & (n_seq - 1)
-    d_down = (off - dest) & (n_seq - 1)
-    in_up = (d_up < half) | ((d_up == half) & low)
-    in_down = (d_down < half) | ((d_down == half) & ~low)
-    groups = jnp.arange(n_grp, dtype=jnp.int32)
-
-    def positions(inside, distance, own_distance):
-        ahead = (inside & (distance > own_distance))[:, :, None]
-        mine = (inside & here)[:, :, None]
-        before = mine & (src[:, :, None] < groups)
-        place = jnp.sum((ahead | before).astype(jnp.int32), axis=1)
-        present = jnp.any(mine & (src[:, :, None] == groups), axis=1)
-        return jnp.where(present, place, -1)
-
-    up = jnp.flip(positions(in_up, d_up, dest)[1 : half + 1], 0)
-    down = positions(in_down, d_down, n_seq - dest)[half:]
-    by_step = jnp.stack([up, down], axis=1).reshape(n_seq, n_grp)
-    same = jnp.any(here[0][:, None] & (src[0][:, None] == groups), axis=0)
-    by_step = jnp.concatenate([by_step, jnp.where(same, groups, -1)[None, :]], axis=0)
-    slot = [(k % spc) + spc * direction for k in range(half) for direction in range(2)]
-    slot[1] = 0
-    slot = jnp.array(slot + [spc], jnp.int32)
-    at_slot = slot[:, None, None] == jnp.arange(half, dtype=jnp.int32)
-    table = jnp.where(at_slot, by_step[:, :, None], -1).reshape(n_seq + 1, n_grp * half)
-    return table, by_step
-
-
-def lists_fit(lists, caps, tok_rows, n_grp, n_seq):
-    half = n_seq // 2
-    owner = lists // tok_rows
-    low = owner // n_seq < n_grp // 2
-    column = owner % n_seq
-    dest = jnp.arange(lists.shape[0], dtype=jnp.int32)[:, None] % n_seq
-    gap = (dest - column) & (n_seq - 1)
-    d_up = jnp.where((gap < half) | ((gap == half) & low), gap, 0)
-    gap = (column - dest) & (n_seq - 1)
-    d_down = jnp.where((gap < half) | ((gap == half) & ~low), gap, 0)
-    least = half - jnp.arange(half, dtype=jnp.int32)
-    limit = jnp.array(caps, jnp.int32)
-    worst = 0
-    for distance in (d_up, d_down):
-        count = jnp.sum((distance[:, None, :] >= least[:, None]).astype(jnp.int32), axis=2)
-        worst = jnp.maximum(worst, jnp.max(count - limit))
-    return worst <= 0
+    gap_up = (dest - column) & (n_seq - 1)
+    gap_down = (column - dest) & (n_seq - 1)
+    d_up = jnp.where((gap_up < half) | ((gap_up == half) & low), gap_up, 0)
+    d_down = jnp.where((gap_down < half) | ((gap_down == half) & ~low), gap_down, 0)
+
+    def count(mask):
+        return jnp.sum(mask.astype(jnp.int32), axis=0, keepdims=True)
+
+    over = jnp.zeros((1, n_experts), jnp.int32)
+    for k, cap in enumerate(caps):
+        if cap < n_grp * (k + 1) - n_grp // 2:
+            for distance in (d_up, d_down):
+                over = jnp.maximum(over, count(distance >= half - k) - cap)
+    bad = jnp.max(over.astype(F32), axis=1, keepdims=True)
+    got[0] = jnp.broadcast_to(jnp.where(bad > 0.5, 0.0, 1.0), got.shape[1:])
+    pl.semaphore_wait(barrier, n_rep - 1)
+
+    def tell(step):
+        return pltpu.make_async_remote_copy(
+            src_ref=got.at[0],
+            dst_ref=got.at[step],
+            send_sem=send_sem.at[step],
+            recv_sem=recv_sem.at[step],
+            device_id={"rep": peer(step)},
+            device_id_type=MESH,
+        )
+
+    for step in range(1, n_rep):
+        tell(step).start()
+
+    local = lists - me * tok_rows
+    mine = (local >= 0) & (local < tok_rows)
+    picked = jnp.max(jnp.where(mine, local, -1), axis=0, keepdims=True)
+    picked_ref[...] = jnp.broadcast_to(picked, picked_ref.shape)
+
+    shape = (n_experts, n_experts)
+    row = iota(shape, 0)
+    turn = row & (spc - 1)
+    chunk = row >> shift(lanes)
+    distance = half - spc * chunk - turn
+    backward = (row >> shift(spc)) & 1
+    rel = jnp.where(backward == 0, distance, jnp.where(distance == half, 0, n_seq - distance))
+    wanted = ((row >> shift(half)) & (n_grp - 1)) * n_seq + ((rel + col) & (n_seq - 1))
+    perm = jnp.where(iota(shape, 1) == wanted, 1.0, 0.0).astype(BF16)
+    hot_t = jnp.where(iota((tok_rows, n_experts), 0) == picked, 1.0, 0.0).astype(BF16)
+    nt = (((1,), (1,)), ((), ()))
+    hot_ref[...] = lax.dot_general(perm, hot_t, nt, preferred_element_type=F32).astype(BF16)
+
+    here = column == col
+    up_gap = (dest - col) & (n_seq - 1)
+    down_gap = (col - dest) & (n_seq - 1)
+    ahead_up = count(d_up > up_gap)
+    ahead_down = count(d_down > down_gap)
+    source = iota((n_grp, n_experts), 0)
+    rows_up = jnp.zeros((n_grp, n_experts), jnp.int32)
+    rows_down, rows_same = rows_up, rows_up
+    for g in range(n_grp):
+        present = count(here & (src == g))
+        goes_up = (up_gap < half) | (up_gap == half) if g < n_grp // 2 else up_gap < half
+        goes_down = down_gap < half if g < n_grp // 2 else (down_gap < half) | (down_gap == half)
+        at_up = jnp.where(goes_up, present, 0)
+        at_down = jnp.where(goes_down, present, 0)
+        ahead_up = ahead_up + at_up
+        ahead_down = ahead_down + at_down
+        rows_up = jnp.where(source == g, at_up * ahead_up, rows_up)
+        rows_down = jnp.where(source == g, at_down * ahead_down, rows_down)
+        rows_same = jnp.where(source == g, present * (g + 1), rows_same)
+
+    n_rows = src_pos_ref.shape[0]
+    shape = (n_rows, n_experts)
+    row = iota(shape, 0)
+    hop = half - (row >> 1)
+    lane = iota(shape, 1)
+    base = grp * n_seq
+
+    def pick(offset, on):
+        wanted = base + ((col + offset) & (n_seq - 1))
+        return jnp.where((lane == wanted) & on, 1.0, 0.0).astype(BF16)
+
+    def take(select, values):
+        return lax.dot_general(select, values.astype(F32).astype(BF16), nt, preferred_element_type=F32)
+
+    stepping = row < n_seq
+    places = take(pick(hop, stepping & ((row & 1) == 0)), rows_up)
+    places = places + take(pick(n_seq - hop, stepping & ((row & 1) == 1)), rows_down)
+    places = places + take(pick(0, row == n_seq), rows_same)
+    src_pos_ref[...] = places.astype(jnp.int32) - 1
+    shape = (n_grp, lanes)
+    spread = jnp.where(iota(shape, 1) >> shift(half) == iota(shape, 0), 1.0, 0.0).astype(BF16)
+    wide = jnp.dot(places.astype(BF16), spread, preferred_element_type=F32).astype(jnp.int32)
+    shape = (n_rows, lanes)
+    row = iota(shape, 0)
+    slot = ((row >> 1) & (spc - 1)) + spc * (row & 1)
+    slot = jnp.where(row == 1, 0, jnp.where(row == n_seq, spc, slot))
+    pos_ref[...] = jnp.where((iota(shape, 1) & (half - 1)) == slot, wide, 0) - 1
+
+    for step in range(1, n_rep):
+        tell(step).wait()
+    flag = got[0]
+    for step in range(1, n_rep):
+        flag = flag * got[step]
+    flag_ref[...] = flag
+
+
+def prepare(dims, tok_rows, caps, lists):
+    n_grp, n_seq, n_rep = dims
+    n_experts = lists.shape[0]
+    n_rows = n_seq + 8
+    lanes = n_grp * (n_seq // 2)
+    vmem = pl.BlockSpec(memory_space=pltpu.VMEM)
+    return pl.pallas_call(
+        functools.partial(prepare_kernel, dims, tok_rows, caps),
+        out_shape=(
+            jax.ShapeDtypeStruct((8, 128), F32),
+            jax.ShapeDtypeStruct((8, n_experts), jnp.int32),
+            jax.ShapeDtypeStruct((n_experts, tok_rows), BF16),
+            jax.ShapeDtypeStruct((n_rows, lanes), jnp.int32),
+            jax.ShapeDtypeStruct((n_rows, n_grp), jnp.int32),
+        ),
+        in_specs=[vmem],
+        out_specs=(vmem,) * 5,
+        scratch_shapes=[
+            pltpu.VMEM((n_rep, 8, 128), F32),
+            pltpu.SemaphoreType.DMA((n_rep,)),
+            pltpu.SemaphoreType.DMA((n_rep,)),
+        ],
+        compiler_params=pltpu.CompilerParams(
+            collective_id=2, has_side_effects=True, vmem_limit_bytes=16 * 1024 * 1024
+        ),
+        name="prepare",
+    )(lists)
 
 
 def body(tokens, token_cot, router_logits, token_lists, w_gate, w_up, w_down):
     n_grp = lax.axis_size("grp")
     n_seq = lax.axis_size("seq")
     half = n_seq // 2
-    grp = lax.axis_index("grp")
     col = lax.axis_index("seq")
     tok_rows, width = tokens.shape
     n_experts, cap = token_lists.shape
     dims = (n_grp, n_seq, width, 128)
 
     token_ids = jnp.arange(tok_rows, dtype=jnp.int32)
-    local = token_lists - (grp * n_seq + col) * tok_rows
-    mine = (local >= 0) & (local < tok_rows)
-    picked = jnp.max(jnp.where(mine, local, -1), axis=1)
-    slots = to_slots(roll_columns(picked.reshape(n_grp, n_seq), col), half)
-    hot = (slots.reshape(n_experts)[:, None] == token_ids).astype(BF16)
-
-    ring_lists = lax.dynamic_slice_in_dim(token_lists, grp * n_seq, n_seq, axis=0)
-    ring_lists = jnp.concatenate([ring_lists, ring_lists], axis=0)
-    ring_lists = lax.dynamic_slice_in_dim(ring_lists, col, n_seq, axis=0)
-    pos, src_pos = ring_positions(ring_lists, tok_rows, n_grp, n_seq, col)
-
     full = tuple(up16(n_grp * k - n_grp // 2) for k in range(1, half + 1))
     usual = usual_caps(n_grp, n_seq)
-    fits = lists_fit(token_lists, usual, tok_rows, n_grp, n_seq)
-    fits = jnp.full((8, 128), fits, F32)
-    n_rep = lax.axis_size("rep")
-    agreed = fits
-    for shift in range(1, n_rep):
-        agreed = agreed * lax.ppermute(fits, "rep", [(i, (i + shift) % n_rep) for i in range(n_rep)])
+    flag, picked, hot, pos, src_pos = prepare((n_grp, n_seq, lax.axis_size("rep")), tok_rows, usual, token_lists)
+    picked = picked[0]
     fin = lax.cond(
-        agreed[0, 0] > 0.5,
+        flag[0, 0] > 0.5,
         functools.partial(exchange, dims, usual, 0),
         functools.partial(exchange, dims, full, 1),
         tokens, token_cot, hot, pos, src_pos, w_gate[0], w_up[0], w_down[0],
@@ -495,7 +586,7 @@
     select = picked[None, :] == token_ids[:, None]
     own_gates = jnp.sum(jnp.where(select, gate_vals, 0.0), axis=0)
     gate_slots = to_slots(roll_columns(own_gates.reshape(n_grp, n_seq), col), half).reshape(n_experts)
-    weight = jnp.where(slots.reshape(n_experts)[:, None] == token_ids, gate_slots[:, None], 0.0)
+    weight = hot.astype(F32) * gate_slots[:, None]
     token_grad = lax.dot_general(
         weight,
         fin[:, :width].astype(F32),

time: 313 us -> 289 us (0.923)
  other arithmetic: 16.6 us -> 0.97 us
  starting transfers between devices: 10.8 us -> 0 us
  Pallas kernels: 275 us -> 282 us
    ppermute x3 -> x0, starting transfers between devices: 10.8 us -> none  [body(): lax.ppermute(fits, 'rep', [(i, (i + shift) % n_rep) for i in range(n_rep)])]
    reduce_sum x2 -> x0, other arithmetic: 9.93 us -> none  [the longest x1 8.76 us: lists_fit(): jnp.sum((distance[:, None, :] >= least[:, None]).astype(jnp.int32), axis=2)]
    pallas_call x0 -> x1, Pallas kernels: none -> 6.61 us  [prepare(): pl.pallas_call(functools.partial(prepare_kernel, dims, tok_rows, caps), o...]
  transfers between devices with their start and end apart: 3 -> 0, of which waited for: 0 -> 0; matrix products, arithmetic and copies ran while one was open for 1% -> 0% of each run, Pallas kernels for 0% -> 0%
where the time goes in v3:
time: 289 us
  Pallas kernels  282 us (98%)
    pallas_call x1, Pallas kernels, exchange(): pl.pallas_call(kernel, out_shape=jax.ShapeDtypeStruct((2, n_grp, half, wi...  276 us
    pallas_call x1, Pallas kernels, prepare(): pl.pallas_call(functools.partial(prepare_kernel, dims, tok_rows, caps), o...  6.61 us

profile of v3, /device:TPU:1, one launch (start us, length us, event | category | flops | bytes accessed | tf_op | source)
XLA Modules:
  0.0 289.2 jit_solution(13223596349218287072)
XLA Ops:
  0.6 0.0 copy-start
  0.7 0.9 copy-done
  1.5 6.6 %prepare.1 = (f32[8,128]{1,0:T(8,128)S(1)}, s32[8,256]{1,0:T(8,128)S(1)}, bf16[256,128]{1,0:T(8,128)(2,1)S(1)}, s32[40,128]{1,0:T(8,128)S(1)}, s32[40,8]{1,0:T(8,128)S(1)}) custom-call(s32[256,128]{1,0:T(8,128)S(1)} %copy-done), custom_call_target="tpu_custom_call" | custom-call | tf_op jit(solution)/shard_map/prepare/pallas_call | solution.py:540
  8.2 0.5 slice.56
  9.3 0.0 copy-start.1
  9.4 276.0 %conditional.1 = (bf16[2,8,16,2176]{3,2,1,0:T(8,128)(2,1)S(1)}) conditional(s32[]{:T(128)} %bitcast.3, (bf16[128,2048]{1,0:T(8,128)(2,1)}, bf16[128,2048]{1,0:T(8,128)(2,1)}, bf16[256,128]{1,0:T(8,128)(2,1)S(1)}, s32[40,128]{1,0:T(8,128)S(1)}, s32[40,8]{1,0:T(8,128)S(1)}, /*index=5*/bf16[2048,384]{1,0:T(8,128)(2,1)}, bf16[2048,384]{1,0:T(8,128)(2,1)}, ...), branch_computations={%region_1.0_spmd, %region_2.3_spmd} | conditional | bytes 8 | solution.py:577
  9.6 275.8 %ring_exchange_0.1 = bf16[2,8,16,2176]{3,2,1,0:T(8,128)(2,1)S(1)} custom-call(bf16[128,2048]{1,0:T(8,128)(2,1)} %get-tuple-element.43.refs_0_, bf16[128,2048]{1,0:T(8,128)(2,1)} %get-tuple-element.44.refs_1_, bf16[256,128]{1,0:T(8,128)(2,1)S(1)} %get-tuple-element.45.refs_2_, s32[40,128]{1,0:T(8,128)S(1)} %get-tuple-element.46.refs_3_, ...), custom_call_target="tpu_custom_call" | custom-call | tf_op jit(solution)/shard_map/cond/branch_1_fun/ring_exchange_0/pallas_call | solution.py:359
  285.3 0.1 slice_reduce_fusion
  285.4 0.1 squeeze.20
  285.5 0.1 squeeze.19
  285.6 0.1 rev.17
  285.7 0.1 slice.63
  285.8 0.1 slice.59
  285.8 0.1 fusion.7
  285.9 0.1 rev.16
  286.0 0.1 concatenate.17
  286.1 0.1 dynamic-slice_convert_fusion
  286.2 0.1 reshape.30
  286.3 0.0 copy-done.1
  286.3 0.7 fusion.2
  287.0 0.1 reshape.27
  287.1 0.1 pad_maximum_fusion.1
  287.2 0.1 constant_dynamic-slice_fusion
  287.2 0.1 slice.53
  287.3 0.1 fusion.6
  287.4 0.1 rev.14
  287.4 0.1 rev.15
  287.5 0.1 maximum_bitcast_fusion
  287.6 0.1 mul.21
  287.7 1.5 convolution_convert_fusion
  (2 shorter events, 0.0 us)
Async XLA Ops:
  0.6 0.9 copy-start
  9.3 276.9 %copy-start.1 = (f32[128,256]{1,0:T(8,128)S(1)}, f32[128,256]{1,0:T(8,128)}, u32[]{:S(2)}) copy-start(f32[128,256]{1,0:T(8,128)} %param.11) | copy-start | bytes 393220

commit v4 on v3

--- a/solution.py
+++ b/solution.py
@@ -11,10 +11,12 @@
 MESH = pl.DeviceIdType.MESH
 BF16 = jnp.bfloat16
 F32 = jnp.float32
-
-
-def up16(n):
-    return -(-n // 16) * 16
+CHUNKS = 4
+GRAIN = 4
+
+
+def to_grain(n):
+    return -(-n // GRAIN) * GRAIN
 
 
 def usual_caps(n_grp, n_seq):
@@ -23,7 +25,7 @@
     for k in range(1, n_seq // 2 + 1):
         slots = n_grp * k - n_grp // 2
         spread = math.sqrt(slots * (total - slots) / (4 * total))
-        caps.append(-(-math.floor(min(slots, slots / 2 + 4.75 * spread)) // 8) * 8)
+        caps.append(-(-math.floor(min(slots, slots / 2 + 4.75 * spread)) // GRAIN) * GRAIN)
     return tuple(max(cap, caps[0]) for cap in caps)
 
 
@@ -35,13 +37,14 @@
 def ring_kernel(dims, caps, ins, fin_ref, scratch):
     n_grp, n_seq, width, tail = dims
     half = n_seq // 2
-    spc = half // 2
+    spc = half // CHUNKS
+    slots = 2 * spc
     wide = width + tail
-    lanes = n_grp * half
+    lanes = n_grp * slots
     x_ref, g_ref, hot_ref, pos_ref, src_pos_ref, wg_hbm, wu_hbm, wd_hbm = ins
     packs, backs = scratch["packs"], (scratch["backs_a"], scratch["backs_b"])
     wg_ref, wu_ref, wd_ref = scratch["wg"], scratch["wu"], scratch["wd"]
-    send_buf, own, fresh, final = scratch["send_buf"], scratch["own"], scratch["fresh"], scratch["final"]
+    send_buf, own, fresh, final, flat = (scratch[name] for name in ("send_buf", "own", "fresh", "final", "flat"))
     gate_scr, up_scr, dx = scratch["gate"], scratch["up"], (scratch["dx_a"], scratch["dx_b"])
     dropped, back_send = scratch["dropped"], scratch["back_send"]
     parts = ((0, width // 2), (width // 2, wide - width // 2))
@@ -78,7 +81,7 @@
         def tile(i, carry):
             cols = tile_cols(i)
             rows = jnp.dot(hot, source[:, cols], preferred_element_type=F32).astype(BF16)
-            send_buf[arr, chunk, :, :, cols] = rows.reshape(n_grp, half, col_tile)
+            send_buf[arr, chunk, :, :, cols] = rows.reshape(n_grp, slots, col_tile)
             return carry
 
         lax.fori_loop(0, n_tiles, tile, 0)
@@ -105,7 +108,7 @@
 
     pick(x_ref, 0, 0)
     pl.semaphore_wait(barrier, n_grp + 1)
-    for chunk, arr in ((0, 0), (0, 1), (1, 0), (1, 1)):
+    for chunk, arr in [(chunk, arr) for chunk in range(CHUNKS) for arr in range(2)]:
         if chunk or arr:
             pick((x_ref, g_ref)[arr], arr, chunk)
         stage_local(arr, chunk).start()
@@ -116,9 +119,9 @@
 
     def send_packet(step, arr, direction):
         if step + 1 < half:
-            dst = packs[step + 1].at[arr, direction, pl.ds(0, caps[step])]
+            dst = packs[step + 1].at[arr, direction, pl.ds(0, caps[step] // GRAIN)]
         else:
-            dst = final.at[arr, pl.ds(direction * cap_last, cap_last)]
+            dst = final.at[arr, pl.ds(direction * cap_last // GRAIN, cap_last // GRAIN)]
         return pltpu.make_async_remote_copy(
             src_ref=packs[step].at[arr, direction],
             dst_ref=dst,
@@ -139,10 +142,12 @@
                 cols = tile_cols(i)
                 mine = own[arr, step // spc, :, :, cols].reshape(lanes, col_tile)
                 rows = jnp.dot(hot, mine, preferred_element_type=F32).astype(BF16)
-                if prev_cap:
-                    fresh[arr, direction, pl.ds(0, prev_cap), cols] = rows[:prev_cap]
+                rows = rows.reshape(cap // GRAIN, GRAIN, col_tile)
+                held = prev_cap // GRAIN
+                if held:
+                    fresh[arr, direction, pl.ds(0, held), :, cols] = rows[:held]
                 if cap > prev_cap:
-                    packs[step][arr, direction, pl.ds(prev_cap, cap - prev_cap), cols] = rows[prev_cap:]
+                    packs[step][arr, direction, pl.ds(held, cap // GRAIN - held), :, cols] = rows[held:]
                 return inner
 
             lax.fori_loop(0, n_tiles, tile, 0)
@@ -158,16 +163,16 @@
 
             def hop(direction, carry, step=step, arr=arr):
                 if step:
-                    prev = pl.ds(0, caps[step - 1])
+                    prev = pl.ds(0, caps[step - 1] // GRAIN)
                     send_packet(step - 1, arr, direction).wait_recv()
-                    packs[step][arr, direction, prev, :] += fresh[arr, direction, prev, :]
+                    packs[step][arr, direction, prev] += fresh[arr, direction, prev]
                 send_packet(step, arr, direction).start()
                 return carry
 
             lax.fori_loop(0, 2, hop, 0)
             if step + 1 < half:
-                if step + 1 == spc:
-                    stage_wait(arr, 1)
+                if (step + 1) % spc == 0:
+                    stage_wait(arr, (step + 1) // spc)
                 make_fresh(step + 1, arr)
 
     same_hot = one_hot_rows(pos_ref[pl.ds(2 * half, 1), :], 16)
@@ -177,21 +182,30 @@
             cols = tile_cols(i)
             mine = own[arr, 0, :, :, cols].reshape(lanes, col_tile)
             rows = jnp.dot(same_hot, mine, preferred_element_type=F32)
-            final[arr, pl.ds(2 * cap_last, 16), cols] = rows.astype(BF16)
+            flat[arr, pl.ds(2 * cap_last, 16), cols] = rows.astype(BF16)
             return inner
 
         lax.fori_loop(0, n_tiles, same_tile, 0)
 
     for copy in weights:
         copy.wait()
-    for direction in range(2):
-        send_packet(half - 1, 0, direction).wait_recv()
-    gate_scr[...] = jnp.dot(final[0], wg_ref[...], preferred_element_type=F32)
-    up_scr[...] = jnp.dot(final[0], wu_ref[...], preferred_element_type=F32)
-    for direction in range(2):
-        send_packet(half - 1, 1, direction).wait_recv()
+    def take_packets(arr):
+        for direction in range(2):
+            send_packet(half - 1, arr, direction).wait_recv()
+
+        def tile(i, carry):
+            cols = tile_cols(i)
+            flat[arr, pl.ds(0, 2 * cap_last), cols] = final[arr, :, :, cols].reshape(2 * cap_last, col_tile)
+            return carry
+
+        lax.fori_loop(0, n_tiles, tile, 0)
+
+    take_packets(0)
+    gate_scr[...] = jnp.dot(flat[0], wg_ref[...], preferred_element_type=F32)
+    up_scr[...] = jnp.dot(flat[0], wu_ref[...], preferred_element_type=F32)
+    take_packets(1)
     nt = (((1,), (1,)), ((), ()))
-    d_hidden = lax.dot_general(final[1], wd_ref[...], nt, preferred_element_type=F32)
+    d_hidden = lax.dot_general(flat[1], wd_ref[...], nt, preferred_element_type=F32)
     gate_pre = gate_scr[...]
     up_pre = up_scr[...]
     sig = jax.nn.sigmoid(gate_pre)
@@ -200,14 +214,16 @@
     gate_grad = jnp.sum(hidden * d_hidden, axis=1, keepdims=True)
     scratch["d_gate"][...] = (d_hidden * up_pre * sig * (1.0 + gate_pre * (1.0 - sig))).astype(BF16)
     scratch["d_up"][...] = (d_hidden * activated).astype(BF16)
-    dx[1][:, width // 2 :] = jnp.broadcast_to(gate_grad, (gate_grad.shape[0], tail)).astype(BF16)
+    n_rows = gate_grad.shape[0]
+    gates = jnp.broadcast_to(gate_grad, (n_rows, tail)).astype(BF16)
+    dx[1][:, :, width // 2 :] = gates.reshape(n_rows // GRAIN, GRAIN, tail)
 
     def send_back(step, part, direction):
         cap = caps[half - 1 - step]
         if step == 0:
-            src = dx[part].at[pl.ds(direction * cap_last, cap_last)]
+            src = dx[part].at[pl.ds(direction * cap_last // GRAIN, cap_last // GRAIN)]
         else:
-            src = backs[part][step - 1].at[direction, pl.ds(0, cap)]
+            src = backs[part][step - 1].at[direction, pl.ds(0, cap // GRAIN)]
         return pltpu.make_async_remote_copy(
             src_ref=src,
             dst_ref=backs[part][step].at[direction],
@@ -223,7 +239,7 @@
             w_rows = tile_cols(i + part * (n_tiles // 2))
             rows = lax.dot_general(scratch["d_gate"][...], wg_ref[w_rows, :], nt, preferred_element_type=F32)
             rows = rows + lax.dot_general(scratch["d_up"][...], wu_ref[w_rows, :], nt, preferred_element_type=F32)
-            dx[part][:, tile_cols(i)] = rows.astype(BF16)
+            dx[part][:, :, tile_cols(i)] = rows.astype(BF16).reshape(n_rows // GRAIN, GRAIN, col_tile)
             return carry
 
         lax.fori_loop(0, n_tiles // 2, dx_tile, 0)
@@ -248,7 +264,7 @@
     def drop(row, cap, rows, slot, part, add=False):
         hot = one_hot_rows(src_pos_ref[pl.ds(row, 1), :n_grp], cap)
         first, size = parts[part]
-        kept = lax.dot_general(hot, rows, tn, preferred_element_type=F32)
+        kept = lax.dot_general(hot, rows.reshape(cap, size), tn, preferred_element_type=F32)
         at = pl.ds(slot * n_grp, n_grp)
         if add:
             kept = kept + dropped[at, pl.ds(first, size)]
@@ -258,11 +274,11 @@
         shape = (lanes, lanes)
         to = lax.broadcasted_iota(jnp.int32, shape, 0)
         frm = lax.broadcasted_iota(jnp.int32, shape, 1)
-        perm = jnp.where((to // half == frm % n_grp) & (to % half == frm // n_grp), 1.0, 0.0).astype(BF16)
+        perm = jnp.where((to // slots == frm % n_grp) & (to % slots == frm // n_grp), 1.0, 0.0).astype(BF16)
 
         def put(cols, size):
             rows = jnp.dot(perm, dropped[:, cols].astype(BF16), preferred_element_type=F32).astype(BF16)
-            back_send[chunk, :, :, cols] = rows.reshape(n_grp, half, size)
+            back_send[chunk, :, :, cols] = rows.reshape(n_grp, slots, size)
 
         def tile(i, carry):
             put(tile_cols(i), col_tile)
@@ -272,26 +288,26 @@
         put(pl.ds(width, tail), tail)
 
     for step in range(half):
-        chunk = 1 if step < spc else 0
         k = half - 1 - step
+        chunk = k // spc
         for part in range(2):
             for direction in range(2):
                 send_back(step, part, direction).wait_recv()
                 if step + 1 < half:
                     send_back(step + 1, part, direction).start()
-            if step == spc:
-                drop(2 * half, 16, dx[part][pl.ds(2 * cap_last, 16), :], spc, part)
+            if k == spc - 1:
+                drop(2 * half, 16, dx[part][pl.ds(2 * cap_last // GRAIN, 16 // GRAIN)], spc, part)
             for direction in range(2):
                 slot = k % spc + (spc if direction and k else 0)
                 drop(2 * k + direction, caps[k], backs[part][step][direction], slot, part, bool(direction and k == 0))
-        if step in (spc - 1, half - 1):
+        if k % spc == 0:
             regroup(chunk)
             home_local(chunk).start()
             for s in range(1, n_grp):
                 home_copy(chunk, s, grp).start()
 
     for arr in range(2):
-        for chunk in range(2):
+        for chunk in range(CHUNKS):
             for s in range(1, n_grp):
                 stage_copy(arr, chunk, s, grp).wait_send()
     for step in range(half):
@@ -299,7 +315,7 @@
             for arr in range(2):
                 send_packet(step, arr, direction).wait_send()
                 send_back(step, arr, direction).wait_send()
-    for chunk in (1, 0):
+    for chunk in reversed(range(CHUNKS)):
         home_local(chunk).wait()
         for s in range(1, n_grp):
             home_copy(chunk, s, grp).wait_send()
@@ -316,7 +332,8 @@
     ff = w_gate.shape[1]
     wide = width + tail
     rows = 2 * caps[-1] + 16
-    lanes = n_grp * half
+    slots = 2 * (half // CHUNKS)
+    lanes = n_grp * slots
     dma = pltpu.SemaphoreType.DMA
     vmem = pl.BlockSpec(memory_space=pltpu.VMEM)
     hbm = pl.BlockSpec(memory_space=pl.ANY)
@@ -324,31 +341,32 @@
         "wg": pltpu.VMEM(w_gate.shape, BF16),
         "wu": pltpu.VMEM(w_up.shape, BF16),
         "wd": pltpu.VMEM(w_down.shape, BF16),
-        "send_buf": pltpu.VMEM((2, 2, n_grp, half, width), BF16),
-        "own": pltpu.VMEM((2, 2, n_grp, half, width), BF16),
-        "packs": [pltpu.VMEM((2, 2, cap, width), BF16) for cap in caps],
-        "fresh": pltpu.VMEM((2, 2, caps[-2], width), BF16),
-        "final": pltpu.VMEM((2, rows, width), BF16),
+        "send_buf": pltpu.VMEM((2, CHUNKS, n_grp, slots, width), BF16),
+        "own": pltpu.VMEM((2, CHUNKS, n_grp, slots, width), BF16),
+        "packs": [pltpu.VMEM((2, 2, cap // GRAIN, GRAIN, width), BF16) for cap in caps],
+        "fresh": pltpu.VMEM((2, 2, caps[-2] // GRAIN, GRAIN, width), BF16),
+        "final": pltpu.VMEM((2, 2 * caps[-1] // GRAIN, GRAIN, width), BF16),
+        "flat": pltpu.VMEM((2, rows, width), BF16),
         "gate": pltpu.VMEM((rows, ff), F32),
         "up": pltpu.VMEM((rows, ff), F32),
         "d_gate": pltpu.VMEM((rows, ff), BF16),
         "d_up": pltpu.VMEM((rows, ff), BF16),
-        "dx_a": pltpu.VMEM((rows, width // 2), BF16),
-        "dx_b": pltpu.VMEM((rows, wide - width // 2), BF16),
-        "backs_a": [pltpu.VMEM((2, cap, width // 2), BF16) for cap in reversed(caps)],
-        "backs_b": [pltpu.VMEM((2, cap, wide - width // 2), BF16) for cap in reversed(caps)],
+        "dx_a": pltpu.VMEM((rows // GRAIN, GRAIN, width // 2), BF16),
+        "dx_b": pltpu.VMEM((rows // GRAIN, GRAIN, wide - width // 2), BF16),
+        "backs_a": [pltpu.VMEM((2, cap // GRAIN, GRAIN, width // 2), BF16) for cap in reversed(caps)],
+        "backs_b": [pltpu.VMEM((2, cap // GRAIN, GRAIN, wide - width // 2), BF16) for cap in reversed(caps)],
         "dropped": pltpu.VMEM((lanes, wide), F32),
-        "back_send": pltpu.VMEM((2, n_grp, half, wide), BF16),
+        "back_send": pltpu.VMEM((CHUNKS, n_grp, slots, wide), BF16),
         "w_sem": dma((3,)),
-        "s1_send": dma((2, 2, n_grp)),
-        "s1_recv": dma((2, 2, n_grp)),
+        "s1_send": dma((2, CHUNKS, n_grp)),
+        "s1_recv": dma((2, CHUNKS, n_grp)),
         "d_send": dma((2, 2, half)),
         "d_recv": dma((2, 2, half)),
         "r_send": dma((2, 2, half)),
         "r_recv": dma((2, 2, half)),
-        "s2_send": dma((2, n_grp)),
-        "s2_recv": dma((2, n_grp)),
-        "loc_sem": dma((3, 2)),
+        "s2_send": dma((CHUNKS, n_grp)),
+        "s2_recv": dma((CHUNKS, n_grp)),
+        "loc_sem": dma((3, CHUNKS)),
     }
     leaves, tree = jax.tree.flatten(scratch, is_leaf=lambda leaf: not isinstance(leaf, (dict, list)))
 
@@ -358,7 +376,7 @@
 
     return pl.pallas_call(
         kernel,
-        out_shape=jax.ShapeDtypeStruct((2, n_grp, half, wide), BF16),
+        out_shape=jax.ShapeDtypeStruct((CHUNKS, n_grp, slots, wide), BF16),
         in_specs=[vmem] * 5 + [hbm] * 3,
         out_specs=vmem,
         scratch_shapes=leaves,
@@ -370,27 +388,19 @@
 
 
 def to_slots(values, half):
-    spc = half // 2
-    first = jnp.concatenate(
-        [jnp.flip(values[:, spc + 1 : half + 1], 1), values[:, :1], values[:, half + 1 : half + spc]], axis=1
-    )
-    second = jnp.concatenate([jnp.flip(values[:, 1 : spc + 1], 1), values[:, half + spc :]], axis=1)
-    return jnp.stack([first, second])
+    n_grp = values.shape[0]
+    ahead = jnp.flip(values[:, 1 : half + 1], 1).reshape(n_grp, CHUNKS, half // CHUNKS)
+    behind = jnp.concatenate([values[:, :1], values[:, half + 1 :]], axis=1).reshape(n_grp, CHUNKS, half // CHUNKS)
+    return jnp.transpose(jnp.concatenate([ahead, behind], axis=2), (1, 0, 2))
 
 
 def from_slots(slots, half):
-    spc = half // 2
-    first, second = slots[0], slots[1]
-    return jnp.concatenate(
-        [
-            first[:, spc : spc + 1],
-            jnp.flip(second[:, :spc], 1),
-            jnp.flip(first[:, :spc], 1),
-            first[:, spc + 1 :],
-            second[:, spc:],
-        ],
-        axis=1,
-    )
+    n_grp = slots.shape[1]
+    spc = half // CHUNKS
+    slots = jnp.transpose(slots, (1, 0, 2))
+    ahead = jnp.flip(slots[:, :, :spc].reshape(n_grp, half), 1)
+    behind = slots[:, :, spc:].reshape(n_grp, half)
+    return jnp.concatenate([behind[:, :1], ahead, behind[:, 1:]], axis=1)
 
 
 def roll_columns(values, start):
@@ -401,8 +411,9 @@
 def prepare_kernel(dims, tok_rows, caps, lists_ref, flag_ref, picked_ref, hot_ref, pos_ref, src_pos_ref, got, send_sem, recv_sem):
     n_grp, n_seq, n_rep = dims
     half = n_seq // 2
-    spc = half // 2
-    lanes = n_grp * half
+    spc = half // CHUNKS
+    slots = 2 * spc
+    lanes = n_grp * slots
     n_experts = lists_ref.shape[0]
     rep, grp, col = lax.axis_index("rep"), lax.axis_index("grp"), lax.axis_index("seq")
     me = grp * n_seq + col
@@ -469,7 +480,7 @@
     distance = half - spc * chunk - turn
     backward = (row >> shift(spc)) & 1
     rel = jnp.where(backward == 0, distance, jnp.where(distance == half, 0, n_seq - distance))
-    wanted = ((row >> shift(half)) & (n_grp - 1)) * n_seq + ((rel + col) & (n_seq - 1))
+    wanted = ((row >> shift(slots)) & (n_grp - 1)) * n_seq + ((rel + col) & (n_seq - 1))
     perm = jnp.where(iota(shape, 1) == wanted, 1.0, 0.0).astype(BF16)
     hot_t = jnp.where(iota((tok_rows, n_experts), 0) == picked, 1.0, 0.0).astype(BF16)
     nt = (((1,), (1,)), ((), ()))
@@ -515,13 +526,13 @@
     places = places + take(pick(0, row == n_seq), rows_same)
     src_pos_ref[...] = places.astype(jnp.int32) - 1
     shape = (n_grp, lanes)
-    spread = jnp.where(iota(shape, 1) >> shift(half) == iota(shape, 0), 1.0, 0.0).astype(BF16)
+    spread = jnp.where(iota(shape, 1) >> shift(slots) == iota(shape, 0), 1.0, 0.0).astype(BF16)
     wide = jnp.dot(places.astype(BF16), spread, preferred_element_type=F32).astype(jnp.int32)
     shape = (n_rows, lanes)
     row = iota(shape, 0)
     slot = ((row >> 1) & (spc - 1)) + spc * (row & 1)
     slot = jnp.where(row == 1, 0, jnp.where(row == n_seq, spc, slot))
-    pos_ref[...] = jnp.where((iota(shape, 1) & (half - 1)) == slot, wide, 0) - 1
+    pos_ref[...] = jnp.where((iota(shape, 1) & (slots - 1)) == slot, wide, 0) - 1
 
     for step in range(1, n_rep):
         tell(step).wait()
@@ -535,7 +546,7 @@
     n_grp, n_seq, n_rep = dims
     n_experts = lists.shape[0]
     n_rows = n_seq + 8
-    lanes = n_grp * (n_seq // 2)
+    lanes = n_grp * 2 * (n_seq // 2 // CHUNKS)
     vmem = pl.BlockSpec(memory_space=pltpu.VMEM)
     return pl.pallas_call(
         functools.partial(prepare_kernel, dims, tok_rows, caps),
@@ -570,7 +581,7 @@
     dims = (n_grp, n_seq, width, 128)
 
     token_ids = jnp.arange(tok_rows, dtype=jnp.int32)
-    full = tuple(up16(n_grp * k - n_grp // 2) for k in range(1, half + 1))
+    full = tuple(to_grain(n_grp * k - n_grp // 2) for k in range(1, half + 1))
     usual = usual_caps(n_grp, n_seq)
     flag, picked, hot, pos, src_pos = prepare((n_grp, n_seq, lax.axis_size("rep")), tok_rows, usual, token_lists)
     picked = picked[0]
@@ -594,7 +605,7 @@
         precision=lax.Precision.HIGHEST,
         preferred_element_type=F32,
     )
-    back_gates = from_slots(fin[:, width].reshape(2, n_grp, half), half)
+    back_gates = from_slots(fin[:, width].reshape(CHUNKS, n_grp, 2 * (half // CHUNKS)), half)
     back_gates = roll_columns(back_gates, lax.rem(n_seq - col, n_seq)).reshape(n_experts).astype(F32)
     logit_grad = jnp.where(select, gate_vals * (1.0 - gate_vals) * back_gates[None, :], 0.0)
     return (token_grad.astype(BF16), logit_grad)

time: 289 us -> 276 us (0.955)
  Pallas kernels: 282 us -> 269 us
    pallas_call x1, Pallas kernels: 276 us -> 262 us  [exchange(): pl.pallas_call(kernel, out_shape=jax.ShapeDtypeStruct((CHUNKS, n_grp, slo...]
where the time goes in v4:
time: 276 us
  Pallas kernels  269 us (97%)
  local copies, waits for them, and re-layouts  3.09 us (1%)
    pallas_call x1, Pallas kernels, exchange(): pl.pallas_call(kernel, out_shape=jax.ShapeDtypeStruct((CHUNKS, n_grp, slo...  262 us
    pallas_call x1, Pallas kernels, prepare(): pl.pallas_call(functools.partial(prepare_kernel, dims, tok_rows, caps), o...  6.61 us

profile of v4, /device:TPU:1, one launch (start us, length us, event | category | flops | bytes accessed | tf_op | source)
XLA Modules:
  0.0 276.2 jit_solution(12412105919593572694)
XLA Ops:
  0.6 0.0 copy-start
  0.7 0.9 copy-done
  1.5 6.6 %prepare.1 = (f32[8,128]{1,0:T(8,128)S(1)}, s32[8,256]{1,0:T(8,128)S(1)}, bf16[256,128]{1,0:T(8,128)(2,1)S(1)}, s32[40,64]{1,0:T(8,128)S(1)}, s32[40,8]{1,0:T(8,128)S(1)}) custom-call(s32[256,128]{1,0:T(8,128)S(1)} %copy-done), custom_call_target="tpu_custom_call" | custom-call | tf_op jit(solution)/shard_map/prepare/pallas_call | solution.py:551
  8.2 0.5 slice.37
  9.3 0.0 copy-start.1
  9.4 262.7 %conditional.1 = (bf16[4,8,8,2176]{3,2,1,0:T(8,128)(2,1)S(1)}) conditional(s32[]{:T(128)} %bitcast.4, (bf16[128,2048]{1,0:T(8,128)(2,1)}, bf16[128,2048]{1,0:T(8,128)(2,1)}, bf16[256,128]{1,0:T(8,128)(2,1)S(1)}, s32[40,64]{1,0:T(8,128)S(1)}, s32[40,8]{1,0:T(8,128)S(1)}, /*index=5*/bf16[2048,384]{1,0:T(8,128)(2,1)}, bf16[2048,384]{1,0:T(8,128)(2,1)}, ...), branch_computations={%region_1.0_spmd, %region_2.3_spmd} | conditional | bytes 8 | solution.py:588
  9.6 262.5 %ring_exchange_0.1 = bf16[4,8,8,2176]{3,2,1,0:T(8,128)(2,1)S(1)} custom-call(bf16[128,2048]{1,0:T(8,128)(2,1)} %get-tuple-element.43.refs_0_, bf16[128,2048]{1,0:T(8,128)(2,1)} %get-tuple-element.44.refs_1_, bf16[256,128]{1,0:T(8,128)(2,1)S(1)} %get-tuple-element.45.refs_2_, s32[40,64]{1,0:T(8,128)S(1)} %get-tuple-element.46.refs_3_, ...), custom_call_target="tpu_custom_call" | custom-call | tf_op jit(solution)/shard_map/cond/branch_1_fun/ring_exchange_0/pallas_call | solution.py:377
  272.1 0.1 slice_reduce_fusion
  272.2 0.1 reshape_squeeze.3
  272.3 0.1 fusion.6
  272.3 0.1 copy.21
  272.5 0.1 copy.23
  272.6 0.1 copy.20
  272.7 0.1 copy.24
  272.8 0.1 copy.22
  272.9 0.1 concatenate.17
  273.0 0.1 dynamic-slice_convert_fusion
  273.1 0.1 reshape.42
  273.1 0.0 copy-done.1
  273.1 0.7 fusion.2
  273.9 0.1 reshape.35
  274.0 0.1 pad_maximum_fusion
  274.0 0.1 constant_dynamic-slice_fusion
  274.1 0.1 slice.36
  274.2 0.1 pad_maximum_fusion.1
  274.3 0.1 copy.17
  274.3 0.1 slice.34
  274.4 0.1 rev.8
  274.5 0.1 copy.16
  274.6 0.1 copy.18
  274.6 0.1 mul.21
  274.7 1.5 convolution_convert_fusion
  (5 shorter events, 0.1 us)
Async XLA Ops:
  0.6 0.9 copy-start
  9.3 263.8 %copy-start.1 = (f32[128,256]{1,0:T(8,128)S(1)}, f32[128,256]{1,0:T(8,128)}, u32[]{:S(2)}) copy-start(f32[128,256]{1,0:T(8,128)} %param.11) | copy-start | bytes 393220

commit v5 on v4

--- a/solution.py
+++ b/solution.py
@@ -13,6 +13,8 @@
 F32 = jnp.float32
 CHUNKS = 4
 GRAIN = 4
+HALVES = 2
+PARTS = 4
 
 
 def to_grain(n):
@@ -34,6 +36,11 @@
     return jnp.where(row_ids == pos_row, 1.0, 0.0).astype(BF16)
 
 
+def part_columns(width, tail):
+    size = width // PARTS
+    return [(part * size, size + (tail if part == PARTS - 1 else 0)) for part in range(PARTS)]
+
+
 def ring_kernel(dims, caps, ins, fin_ref, scratch):
     n_grp, n_seq, width, tail = dims
     half = n_seq // 2
@@ -42,16 +49,16 @@
     wide = width + tail
     lanes = n_grp * slots
     x_ref, g_ref, hot_ref, pos_ref, src_pos_ref, wg_hbm, wu_hbm, wd_hbm = ins
-    packs, backs = scratch["packs"], (scratch["backs_a"], scratch["backs_b"])
+    packs, backs, dx = scratch["packs"], scratch["backs"], scratch["dx"]
     wg_ref, wu_ref, wd_ref = scratch["wg"], scratch["wu"], scratch["wd"]
     send_buf, own, fresh, final, flat = (scratch[name] for name in ("send_buf", "own", "fresh", "final", "flat"))
-    gate_scr, up_scr, dx = scratch["gate"], scratch["up"], (scratch["dx_a"], scratch["dx_b"])
+    gate_scr, up_scr = scratch["gate"], scratch["up"]
     dropped, back_send = scratch["dropped"], scratch["back_send"]
-    parts = ((0, width // 2), (width // 2, wide - width // 2))
+    parts = part_columns(width, tail)
     grp = lax.axis_index("grp")
     col = lax.axis_index("seq")
     cap_last = caps[half - 1]
-    col_tile = min(width // 2, 512)
+    col_tile = min(width // PARTS, 512)
     n_tiles = width // col_tile
 
     def tile_cols(i):
@@ -117,21 +124,24 @@
     for copy in weights:
         copy.start()
 
-    def send_packet(step, arr, direction):
+    half_tiles = n_tiles // HALVES
+
+    def send_packet(step, stream, direction):
         if step + 1 < half:
-            dst = packs[step + 1].at[arr, direction, pl.ds(0, caps[step] // GRAIN)]
+            dst = packs[step + 1].at[stream, direction, pl.ds(0, caps[step] // GRAIN)]
         else:
-            dst = final.at[arr, pl.ds(direction * cap_last // GRAIN, cap_last // GRAIN)]
+            dst = final.at[stream, pl.ds(direction * cap_last // GRAIN, cap_last // GRAIN)]
         return pltpu.make_async_remote_copy(
-            src_ref=packs[step].at[arr, direction],
+            src_ref=packs[step].at[stream, direction],
             dst_ref=dst,
-            send_sem=scratch["d_send"].at[arr, direction, step],
-            recv_sem=scratch["d_recv"].at[arr, direction, step],
+            send_sem=scratch["d_send"].at[stream, direction, step],
+            recv_sem=scratch["d_recv"].at[stream, direction, step],
             device_id={"seq": neighbour(direction)},
             device_id_type=MESH,
         )
 
-    def make_fresh(step, arr):
+    def make_fresh(step, stream):
+        arr, piece = divmod(stream, HALVES)
         cap = caps[step]
         prev_cap = caps[step - 1] if step else 0
 
@@ -140,40 +150,43 @@
 
             def tile(i, inner):
                 cols = tile_cols(i)
-                mine = own[arr, step // spc, :, :, cols].reshape(lanes, col_tile)
+                from_cols = tile_cols(i + piece * half_tiles)
+                mine = own[arr, step // spc, :, :, from_cols].reshape(lanes, col_tile)
                 rows = jnp.dot(hot, mine, preferred_element_type=F32).astype(BF16)
                 rows = rows.reshape(cap // GRAIN, GRAIN, col_tile)
                 held = prev_cap // GRAIN
                 if held:
-                    fresh[arr, direction, pl.ds(0, held), :, cols] = rows[:held]
+                    fresh[stream, direction, pl.ds(0, held), :, cols] = rows[:held]
                 if cap > prev_cap:
-                    packs[step][arr, direction, pl.ds(held, cap // GRAIN - held), :, cols] = rows[held:]
+                    packs[step][stream, direction, pl.ds(held, cap // GRAIN - held), :, cols] = rows[held:]
                 return inner
 
-            lax.fori_loop(0, n_tiles, tile, 0)
+            lax.fori_loop(0, half_tiles, tile, 0)
             return carry
 
         lax.fori_loop(0, 2, one, 0)
 
     for step in range(half):
-        for arr in range(2):
+        for stream in range(2 * HALVES):
+            arr, piece = divmod(stream, HALVES)
             if step == 0:
-                stage_wait(arr, 0)
-                make_fresh(0, arr)
-
-            def hop(direction, carry, step=step, arr=arr):
+                if piece == 0:
+                    stage_wait(arr, 0)
+                make_fresh(0, stream)
+
+            def hop(direction, carry, step=step, stream=stream):
                 if step:
                     prev = pl.ds(0, caps[step - 1] // GRAIN)
-                    send_packet(step - 1, arr, direction).wait_recv()
-                    packs[step][arr, direction, prev] += fresh[arr, direction, prev]
-                send_packet(step, arr, direction).start()
+                    send_packet(step - 1, stream, direction).wait_recv()
+                    packs[step][stream, direction, prev] += fresh[stream, direction, prev]
+                send_packet(step, stream, direction).start()
                 return carry
 
             lax.fori_loop(0, 2, hop, 0)
             if step + 1 < half:
-                if (step + 1) % spc == 0:
+                if (step + 1) % spc == 0 and piece == 0:
                     stage_wait(arr, (step + 1) // spc)
-                make_fresh(step + 1, arr)
+                make_fresh(step + 1, stream)
 
     same_hot = one_hot_rows(pos_ref[pl.ds(2 * half, 1), :], 16)
     for arr in range(2):
@@ -190,15 +203,17 @@
     for copy in weights:
         copy.wait()
     def take_packets(arr):
-        for direction in range(2):
-            send_packet(half - 1, arr, direction).wait_recv()
-
-        def tile(i, carry):
-            cols = tile_cols(i)
-            flat[arr, pl.ds(0, 2 * cap_last), cols] = final[arr, :, :, cols].reshape(2 * cap_last, col_tile)
-            return carry
-
-        lax.fori_loop(0, n_tiles, tile, 0)
+        for piece in range(HALVES):
+            stream = arr * HALVES + piece
+            for direction in range(2):
+                send_packet(half - 1, stream, direction).wait_recv()
+
+            def tile(i, carry, stream=stream, piece=piece):
+                rows = final[stream, :, :, tile_cols(i)].reshape(2 * cap_last, col_tile)
+                flat[arr, pl.ds(0, 2 * cap_last), tile_cols(i + piece * half_tiles)] = rows
+                return carry
+
+            lax.fori_loop(0, half_tiles, tile, 0)
 
     take_packets(0)
     gate_scr[...] = jnp.dot(flat[0], wg_ref[...], preferred_element_type=F32)
@@ -216,7 +231,7 @@
     scratch["d_up"][...] = (d_hidden * activated).astype(BF16)
     n_rows = gate_grad.shape[0]
     gates = jnp.broadcast_to(gate_grad, (n_rows, tail)).astype(BF16)
-    dx[1][:, :, width // 2 :] = gates.reshape(n_rows // GRAIN, GRAIN, tail)
+    dx[PARTS - 1][:, :, width // PARTS :] = gates.reshape(n_rows // GRAIN, GRAIN, tail)
 
     def send_back(step, part, direction):
         cap = caps[half - 1 - step]
@@ -233,16 +248,16 @@
             device_id_type=MESH,
         )
 
-    for part in range(2):
+    for part in range(PARTS):
 
         def dx_tile(i, carry, part=part):
-            w_rows = tile_cols(i + part * (n_tiles // 2))
+            w_rows = tile_cols(i + part * (n_tiles // PARTS))
             rows = lax.dot_general(scratch["d_gate"][...], wg_ref[w_rows, :], nt, preferred_element_type=F32)
             rows = rows + lax.dot_general(scratch["d_up"][...], wu_ref[w_rows, :], nt, preferred_element_type=F32)
             dx[part][:, :, tile_cols(i)] = rows.astype(BF16).reshape(n_rows // GRAIN, GRAIN, col_tile)
             return carry
 
-        lax.fori_loop(0, n_tiles // 2, dx_tile, 0)
+        lax.fori_loop(0, n_tiles // PARTS, dx_tile, 0)
         for direction in range(2):
             send_back(0, part, direction).start()
 
@@ -290,7 +305,7 @@
     for step in range(half):
         k = half - 1 - step
         chunk = k // spc
-        for part in range(2):
+        for part in range(PARTS):
             for direction in range(2):
                 send_back(step, part, direction).wait_recv()
                 if step + 1 < half:
@@ -312,9 +327,10 @@
                 stage_copy(arr, chunk, s, grp).wait_send()
     for step in range(half):
         for direction in range(2):
-            for arr in range(2):
-                send_packet(step, arr, direction).wait_send()
-                send_back(step, arr, direction).wait_send()
+            for stream in range(2 * HALVES):
+                send_packet(step, stream, direction).wait_send()
+            for part in range(PARTS):
+                send_back(step, part, direction).wait_send()
     for chunk in reversed(range(CHUNKS)):
         home_local(chunk).wait()
         for s in range(1, n_grp):
@@ -334,6 +350,7 @@
     rows = 2 * caps[-1] + 16
     slots = 2 * (half // CHUNKS)
     lanes = n_grp * slots
+    streams, piece, parts = 2 * HALVES, width // HALVES, part_columns(width, tail)
     dma = pltpu.SemaphoreType.DMA
     vmem = pl.BlockSpec(memory_space=pltpu.VMEM)
     hbm = pl.BlockSpec(memory_space=pl.ANY)
@@ -343,27 +360,27 @@
         "wd": pltpu.VMEM(w_down.shape, BF16),
         "send_buf": pltpu.VMEM((2, CHUNKS, n_grp, slots, width), BF16),
         "own": pltpu.VMEM((2, CHUNKS, n_grp, slots, width), BF16),
-        "packs": [pltpu.VMEM((2, 2, cap // GRAIN, GRAIN, width), BF16) for cap in caps],
-        "fresh": pltpu.VMEM((2, 2, caps[-2] // GRAIN, GRAIN, width), BF16),
-        "final": pltpu.VMEM((2, 2 * caps[-1] // GRAIN, GRAIN, width), BF16),
+        "packs": [pltpu.VMEM((streams, 2, cap // GRAIN, GRAIN, piece), BF16) for cap in caps],
+        "fresh": pltpu.VMEM((streams, 2, caps[-2] // GRAIN, GRAIN, piece), BF16),
+        "final": pltpu.VMEM((streams, 2 * caps[-1] // GRAIN, GRAIN, piece), BF16),
         "flat": pltpu.VMEM((2, rows, width), BF16),
         "gate": pltpu.VMEM((rows, ff), F32),
         "up": pltpu.VMEM((rows, ff), F32),
         "d_gate": pltpu.VMEM((rows, ff), BF16),
         "d_up": pltpu.VMEM((rows, ff), BF16),
-        "dx_a": pltpu.VMEM((rows // GRAIN, GRAIN, width // 2), BF16),
-        "dx_b": pltpu.VMEM((rows // GRAIN, GRAIN, wide - width // 2), BF16),
-        "backs_a": [pltpu.VMEM((2, cap // GRAIN, GRAIN, width // 2), BF16) for cap in reversed(caps)],
-        "backs_b": [pltpu.VMEM((2, cap // GRAIN, GRAIN, wide - width // 2), BF16) for cap in reversed(caps)],
+        "dx": [pltpu.VMEM((rows // GRAIN, GRAIN, size), BF16) for _, size in parts],
+        "backs": [
+            [pltpu.VMEM((2, cap // GRAIN, GRAIN, size), BF16) for cap in reversed(caps)] for _, size in parts
+        ],
         "dropped": pltpu.VMEM((lanes, wide), F32),
         "back_send": pltpu.VMEM((CHUNKS, n_grp, slots, wide), BF16),
         "w_sem": dma((3,)),
         "s1_send": dma((2, CHUNKS, n_grp)),
         "s1_recv": dma((2, CHUNKS, n_grp)),
-        "d_send": dma((2, 2, half)),
-        "d_recv": dma((2, 2, half)),
-        "r_send": dma((2, 2, half)),
-        "r_recv": dma((2, 2, half)),
+        "d_send": dma((streams, 2, half)),
+        "d_recv": dma((streams, 2, half)),
+        "r_send": dma((PARTS, 2, half)),
+        "r_recv": dma((PARTS, 2, half)),
         "s2_send": dma((CHUNKS, n_grp)),
         "s2_recv": dma((CHUNKS, n_grp)),
         "loc_sem": dma((3, CHUNKS)),

time: 276 us -> 275 us (level)
  no operation moved by 1% of the time
where the time goes in v5:
time: 275 us
  Pallas kernels  267 us (97%)
  local copies, waits for them, and re-layouts  3.09 us (1%)
    pallas_call x1, Pallas kernels, exchange(): pl.pallas_call(kernel, out_shape=jax.ShapeDtypeStruct((CHUNKS, n_grp, slo...  261 us
    pallas_call x1, Pallas kernels, prepare(): pl.pallas_call(functools.partial(prepare_kernel, dims, tok_rows, caps), o...  6.61 us

profile of v5, /device:TPU:1, one launch (start us, length us, event | category | flops | bytes accessed | tf_op | source)
XLA Modules:
  0.0 274.6 jit_solution(13140223338786190086)
XLA Ops:
  0.6 0.0 copy-start
  0.7 0.9 copy-done
  1.5 6.6 %prepare.1 = (f32[8,128]{1,0:T(8,128)S(1)}, s32[8,256]{1,0:T(8,128)S(1)}, bf16[256,128]{1,0:T(8,128)(2,1)S(1)}, s32[40,64]{1,0:T(8,128)S(1)}, s32[40,8]{1,0:T(8,128)S(1)}) custom-call(s32[256,128]{1,0:T(8,128)S(1)} %copy-done), custom_call_target="tpu_custom_call" | custom-call | tf_op jit(solution)/shard_map/prepare/pallas_call | solution.py:568
  8.2 0.5 slice.37
  9.3 0.0 copy-start.1
  9.4 261.1 %conditional.1 = (bf16[4,8,8,2176]{3,2,1,0:T(8,128)(2,1)S(1)}) conditional(s32[]{:T(128)} %bitcast.4, (bf16[128,2048]{1,0:T(8,128)(2,1)}, bf16[128,2048]{1,0:T(8,128)(2,1)}, bf16[256,128]{1,0:T(8,128)(2,1)S(1)}, s32[40,64]{1,0:T(8,128)S(1)}, s32[40,8]{1,0:T(8,128)S(1)}, /*index=5*/bf16[2048,384]{1,0:T(8,128)(2,1)}, bf16[2048,384]{1,0:T(8,128)(2,1)}, ...), branch_computations={%region_1.0_spmd, %region_2.3_spmd} | conditional | bytes 8 | solution.py:605
  9.6 260.8 %ring_exchange_0.1 = bf16[4,8,8,2176]{3,2,1,0:T(8,128)(2,1)S(1)} custom-call(bf16[128,2048]{1,0:T(8,128)(2,1)} %get-tuple-element.43.refs_0_, bf16[128,2048]{1,0:T(8,128)(2,1)} %get-tuple-element.44.refs_1_, bf16[256,128]{1,0:T(8,128)(2,1)S(1)} %get-tuple-element.45.refs_2_, s32[40,64]{1,0:T(8,128)S(1)} %get-tuple-element.46.refs_3_, ...), custom_call_target="tpu_custom_call" | custom-call | tf_op jit(solution)/shard_map/cond/branch_1_fun/ring_exchange_0/pallas_call | solution.py:394
  270.4 0.1 slice_reduce_fusion
  270.5 0.1 reshape_squeeze.3
  270.6 0.1 fusion.6
  270.7 0.1 copy.21
  270.8 0.1 copy.23
  270.9 0.1 copy.20
  271.1 0.1 copy.24
  271.1 0.1 copy.22
  271.2 0.1 concatenate.17
  271.3 0.1 dynamic-slice_convert_fusion
  271.4 0.1 reshape.42
  271.5 0.0 copy-done.1
  271.5 0.7 fusion.2
  272.2 0.1 reshape.35
  272.3 0.1 pad_maximum_fusion
  272.4 0.1 constant_dynamic-slice_fusion
  272.5 0.1 slice.36
  272.5 0.1 pad_maximum_fusion.1
  272.6 0.1 copy.17
  272.7 0.1 slice.34
  272.8 0.1 rev.8
  272.8 0.1 copy.16
  272.9 0.1 copy.18
  273.0 0.1 mul.21
  273.1 1.5 convolution_convert_fusion
  (5 shorter events, 0.1 us)
Async XLA Ops:
  0.6 0.9 copy-start
  9.3 262.2 %copy-start.1 = (f32[128,256]{1,0:T(8,128)S(1)}, f32[128,256]{1,0:T(8,128)}, u32[]{:S(2)}) copy-start(f32[128,256]{1,0:T(8,128)} %param.11) | copy-start | bytes 393220
